TPU v7x, 32 devices: a whole 2x2x4 slice. The times are simulated.
32 devices in a mesh: dp: 8 (over y, x, core), tensor: 4 (over z).
Axes of the slice: x: 2, y: 2, z: 4, core: 2. Of those that a mesh axis runs over, the one named last changes fastest.
Arguments:
- tokens: bfloat16 [16384, 2048], P(('dp', 'tensor')), may hold values from -6 to 6
- w_query: bfloat16 [2048, 2048], P('dp', 'tensor'), may hold values from -0.125 to 0.125
- w_key: bfloat16 [2048, 2048], P('dp', 'tensor'), may hold values from -0.125 to 0.125
- w_value: bfloat16 [2048, 2048], P('dp', 'tensor'), may hold values from -0.125 to 0.125
- w_output: bfloat16 [2048, 2048], P('dp', 'tensor'), may hold values from -0.5 to 0.5
- attn_gain: bfloat16 [2048], P('dp'), may hold values from 0.099609375 to 1.8984375
- w_gate: bfloat16 [2048, 8192], P('dp', 'tensor'), may hold values from -0.125 to 0.125
- w_up: bfloat16 [2048, 8192], P('dp', 'tensor'), may hold values from -0.125 to 0.125
- w_down: bfloat16 [2048, 8192], P('dp', 'tensor'), may hold values from -0.0625 to 0.0625
- mlp_gain: bfloat16 [2048], P('dp'), may hold values from 0.099609375 to 1.8984375
- cotangent: bfloat16 [16384, 2048], P(('dp', 'tensor')), may hold values from -6 to 6
Outputs:
- block_out: bfloat16 [16384, 2048], P(('dp', 'tensor'))
- grad_tokens: bfloat16 [16384, 2048], P(('dp', 'tensor'))
- grad_query: float32 [2048, 2048], P('dp', 'tensor')
- grad_key: float32 [2048, 2048], P('dp', 'tensor')
- grad_value: float32 [2048, 2048], P('dp', 'tensor')
- grad_output: float32 [2048, 2048], P('dp', 'tensor')
- grad_attn_gain: float32 [2048], P(('dp', 'tensor'))
- grad_gate: float32 [2048, 8192], P('dp', 'tensor')
- grad_up: float32 [2048, 8192], P('dp', 'tensor')
- grad_down: float32 [2048, 8192], P('dp', 'tensor')
- grad_mlp_gain: float32 [2048], P(('dp', 'tensor'))
All inputs are finite; a program needn't handle non-finite values.
Results may differ from a plain program's by a relative error of at most 0.018.
Values may be sent and summed in bfloat16 or wider, within the bound.
No kernel may reach another device: no remote copies, remote signals or barrier semaphores. Data moves between devices by JAX's collectives and lax.ppermute only.
A program may use at most 256 MiB of HBM per device.

v0:
```python
import jax
import jax.numpy as jnp
from jax import lax
from jax.sharding import PartitionSpec as P

HEAD = 64
LEN = 512


eps = 1e-05
rope_base = 130000.0


def tables(rows):
    half = HEAD // 2
    places = (jnp.arange(rows) % LEN).astype(jnp.float32)
    freqs = rope_base ** (-2.0 * jnp.arange(half).astype(jnp.float32) / HEAD)
    angles = places[:, None] * freqs[None, :]
    return (jnp.cos(angles)[:, None, :], jnp.sin(angles)[:, None, :])


def rotate(values, cosine, sine):
    half = values.shape[-1] // 2
    first = values[..., :half]
    second = values[..., half:]
    return jnp.concatenate(
        [first * cosine - second * sine, second * cosine + first * sine], axis=-1
    )


def contract_rows(left, right):
    return lax.dot_general(
        left, right, (((0,), (0,)), ((), ())), preferred_element_type=jnp.float32
    )


def contract_cols(left, right):
    return lax.dot_general(
        left, right, (((1,), (1,)), ((), ())), preferred_element_type=jnp.float32
    )


def causal_scores(query_seq, key_seq):
    scores = jnp.einsum("qhd,khd->hqk", query_seq, key_seq, preferred_element_type=jnp.float32)
    scores = scores * HEAD ** (-0.5)
    length = query_seq.shape[0]
    allowed = jnp.arange(length)[:, None] >= jnp.arange(length)[None, :]
    return jnp.where(allowed[None], scores, -1e30)


def attend_forward(block):
    query_seq, key_seq, value_seq = block
    scores = causal_scores(query_seq, key_seq)
    top = jnp.max(scores, axis=-1, keepdims=True)
    expo = jnp.exp(scores - top)
    total = jnp.sum(expo, axis=-1, keepdims=True)
    probs = (expo / total).astype(jnp.bfloat16)
    attended = jnp.einsum("hqk,khd->qhd", probs, value_seq, preferred_element_type=jnp.float32)
    return (attended, top + jnp.log(total))


def attend_backward(block):
    query_seq, key_seq, value_seq, log_total, grad_seq = block
    scores = causal_scores(query_seq, key_seq)
    probs = jnp.exp(scores - log_total)
    grad_probs = jnp.einsum("qhd,khd->hqk", grad_seq, value_seq, preferred_element_type=jnp.float32)
    inner = jnp.sum(probs * grad_probs, axis=-1, keepdims=True)
    grad_scores = (probs * (grad_probs - inner)).astype(jnp.bfloat16)
    factor = HEAD ** (-0.5)
    grad_query = (
        jnp.einsum("hqk,khd->qhd", grad_scores, key_seq, preferred_element_type=jnp.float32)
        * factor
    )
    grad_key = (
        jnp.einsum("hqk,qhd->khd", grad_scores, query_seq, preferred_element_type=jnp.float32)
        * factor
    )
    grad_value = jnp.einsum(
        "hqk,qhd->khd", probs.astype(jnp.bfloat16), grad_seq, preferred_element_type=jnp.float32
    )
    return (grad_query, grad_key, grad_value)


def norm_back(grad_normed, source, inverse, gain):
    scaled = grad_normed * gain
    inner = jnp.mean(scaled * source, axis=-1, keepdims=True)
    grad_source = inverse * scaled - source * inverse**3 * inner
    grad_gain = jnp.sum(grad_normed * source * inverse, axis=0)
    return (grad_source, grad_gain)


def local(
    tokens, w_query, w_key, w_value, w_output, attn_gain, w_gate, w_up, w_down, mlp_gain, cotangent
):
    query_full, key_full, value_full, output_full, attn_scale = (
        lax.all_gather(w_query, "dp", axis=0, tiled=True),
        lax.all_gather(w_key, "dp", axis=0, tiled=True),
        lax.all_gather(w_value, "dp", axis=0, tiled=True),
        lax.all_gather(w_output, "dp", axis=0, tiled=True),
        lax.all_gather(attn_gain, "dp", axis=0, tiled=True),
    )
    gate_full, up_full, down_full, mlp_scale = (
        lax.all_gather(w_gate, "dp", axis=0, tiled=True),
        lax.all_gather(w_up, "dp", axis=0, tiled=True),
        lax.all_gather(w_down, "dp", axis=0, tiled=True),
        lax.all_gather(mlp_gain, "dp", axis=0, tiled=True),
    )
    attn_scale = attn_scale.astype(jnp.float32)
    mlp_scale = mlp_scale.astype(jnp.float32)
    source = tokens.astype(jnp.float32)
    inverse_one = lax.rsqrt(jnp.mean(source * source, axis=-1, keepdims=True) + eps)
    normed_one = (source * inverse_one * attn_scale).astype(jnp.bfloat16)
    gathered_one = lax.all_gather(normed_one, "tensor", axis=0, tiled=True)
    rows = gathered_one.shape[0]
    local_heads = query_full.shape[1] // HEAD
    seq_count = rows // LEN
    cosine, sine = tables(rows)

    def by_seq(values):
        return values.reshape(seq_count, LEN, local_heads, HEAD)

    queries = jnp.dot(gathered_one, query_full, preferred_element_type=jnp.float32).reshape(
        rows, local_heads, HEAD
    )
    keys = jnp.dot(gathered_one, key_full, preferred_element_type=jnp.float32).reshape(
        rows, local_heads, HEAD
    )
    values = jnp.dot(gathered_one, value_full, preferred_element_type=jnp.float32).astype(
        jnp.bfloat16
    )
    query_rot = rotate(queries, cosine, sine).astype(jnp.bfloat16)
    key_rot = rotate(keys, cosine, sine).astype(jnp.bfloat16)
    attended, log_total = lax.map(
        attend_forward, (by_seq(query_rot), by_seq(key_rot), by_seq(values))
    )
    mixed_heads = attended.reshape(rows, local_heads * HEAD).astype(jnp.bfloat16)
    part = mixed_heads
    attn_branch = lax.psum_scatter(
        contract_cols(part, output_full), "tensor", scatter_dimension=0, tiled=True
    )
    hidden = source + attn_branch
    inverse_two = lax.rsqrt(jnp.mean(hidden * hidden, axis=-1, keepdims=True) + eps)
    normed_two = (hidden * inverse_two * mlp_scale).astype(jnp.bfloat16)
    gathered_two = lax.all_gather(normed_two, "tensor", axis=0, tiled=True)
    gate = jnp.dot(gathered_two, gate_full, preferred_element_type=jnp.float32)
    up = jnp.dot(gathered_two, up_full, preferred_element_type=jnp.float32)
    sigma = jax.nn.sigmoid(gate)
    swish = gate * sigma
    activ = (swish * up).astype(jnp.bfloat16)
    part = activ
    mlp_branch = lax.psum_scatter(
        contract_cols(part, down_full).astype(jnp.bfloat16),
        "tensor",
        scatter_dimension=0,
        tiled=True,
    ).astype(jnp.float32)
    block_out = (hidden + mlp_branch).astype(jnp.bfloat16)
    gate_back, up_back, down_back = (
        lax.all_gather(w_gate, "dp", axis=0, tiled=True),
        lax.all_gather(w_up, "dp", axis=0, tiled=True),
        lax.all_gather(w_down, "dp", axis=0, tiled=True),
    )
    grad_out_rows = lax.all_gather(cotangent, "tensor", axis=0, tiled=True)
    grad_activ = jnp.dot(grad_out_rows, down_back, preferred_element_type=jnp.float32)
    grad_gate_pre = (grad_activ * up * sigma * (1.0 + gate * (1.0 - sigma))).astype(jnp.bfloat16)
    grad_up_pre = (grad_activ * swish).astype(jnp.bfloat16)
    grad_down_w = contract_rows(grad_out_rows, activ)
    grad_gate_w = contract_rows(gathered_two, grad_gate_pre)
    grad_up_w = contract_rows(gathered_two, grad_up_pre)
    grad_normed_two = lax.psum_scatter(
        contract_cols(grad_gate_pre, gate_back) + contract_cols(grad_up_pre, up_back),
        "tensor",
        scatter_dimension=0,
        tiled=True,
    )
    grad_hidden_norm, grad_mlp_gain = norm_back(grad_normed_two, hidden, inverse_two, mlp_scale)
    grad_hidden = cotangent.astype(jnp.float32) + grad_hidden_norm
    grad_branch = grad_hidden.astype(jnp.bfloat16)
    grad_branch_rows = lax.all_gather(grad_branch, "tensor", axis=0, tiled=True)
    grad_mixed = jnp.dot(grad_branch_rows, output_full, preferred_element_type=jnp.float32).astype(
        jnp.bfloat16
    )
    grad_output_w = contract_rows(grad_branch_rows, mixed_heads)
    grad_query_rot, grad_key_rot, grad_value_seq = lax.map(
        attend_backward,
        (by_seq(query_rot), by_seq(key_rot), by_seq(values), log_total, by_seq(grad_mixed)),
    )
    grad_q_pre = rotate(grad_query_rot.reshape(rows, local_heads, HEAD), cosine, -sine)
    grad_q_pre = grad_q_pre.reshape(rows, local_heads * HEAD).astype(jnp.bfloat16)
    grad_k_pre = rotate(grad_key_rot.reshape(rows, local_heads, HEAD), cosine, -sine)
    grad_k_pre = grad_k_pre.reshape(rows, local_heads * HEAD).astype(jnp.bfloat16)
    grad_v_pre = grad_value_seq.reshape(rows, local_heads * HEAD).astype(jnp.bfloat16)
    grad_query_w = contract_rows(gathered_one, grad_q_pre)
    grad_key_w = contract_rows(gathered_one, grad_k_pre)
    grad_value_w = contract_rows(gathered_one, grad_v_pre)
    total = contract_cols(grad_q_pre, query_full) + contract_cols(grad_k_pre, key_full)
    grad_normed_one = lax.psum_scatter(
        (total + contract_cols(grad_v_pre, value_full)).astype(jnp.bfloat16),
        "tensor",
        scatter_dimension=0,
        tiled=True,
    ).astype(jnp.float32)
    grad_source_norm, grad_attn_gain = norm_back(grad_normed_one, source, inverse_one, attn_scale)
    grad_tokens = (grad_hidden + grad_source_norm).astype(jnp.bfloat16)
    grad_query, grad_key, grad_value, grad_output = (
        lax.psum_scatter(
            grad_query_w.astype(jnp.bfloat16), "dp", scatter_dimension=0, tiled=True
        ).astype(jnp.float32),
        lax.psum_scatter(
            grad_key_w.astype(jnp.bfloat16), "dp", scatter_dimension=0, tiled=True
        ).astype(jnp.float32),
        lax.psum_scatter(
            grad_value_w.astype(jnp.bfloat16), "dp", scatter_dimension=0, tiled=True
        ).astype(jnp.float32),
        lax.psum_scatter(
            grad_output_w.astype(jnp.bfloat16), "dp", scatter_dimension=0, tiled=True
        ).astype(jnp.float32),
    )
    grad_gate, grad_up, grad_down = (
        lax.psum_scatter(
            grad_gate_w.astype(jnp.bfloat16), "dp", scatter_dimension=0, tiled=True
        ).astype(jnp.float32),
        lax.psum_scatter(
            grad_up_w.astype(jnp.bfloat16), "dp", scatter_dimension=0, tiled=True
        ).astype(jnp.float32),
        lax.psum_scatter(
            grad_down_w.astype(jnp.bfloat16), "dp", scatter_dimension=0, tiled=True
        ).astype(jnp.float32),
    )
    attn_gain_sum, mlp_gain_sum = (
        lax.psum_scatter(grad_attn_gain, ("dp", "tensor"), scatter_dimension=0, tiled=True),
        lax.psum_scatter(grad_mlp_gain, ("dp", "tensor"), scatter_dimension=0, tiled=True),
    )
    return (
        block_out,
        grad_tokens,
        grad_query,
        grad_key,
        grad_value,
        grad_output,
        attn_gain_sum,
        grad_gate,
        grad_up,
        grad_down,
        mlp_gain_sum,
    )


def solution(mesh):
    in_specs = (
        P(("dp", "tensor"), None),
        P("dp", "tensor"),
        P("dp", "tensor"),
        P("dp", "tensor"),
        P("dp", "tensor"),
        P("dp"),
        P("dp", "tensor"),
        P("dp", "tensor"),
        P("dp", "tensor"),
        P("dp"),
        P(("dp", "tensor"), None),
    )
    out_specs = (
        P(("dp", "tensor"), None),
        P(("dp", "tensor"), None),
        P("dp", "tensor"),
        P("dp", "tensor"),
        P("dp", "tensor"),
        P("dp", "tensor"),
        P(("dp", "tensor")),
        P("dp", "tensor"),
        P("dp", "tensor"),
        P("dp", "tensor"),
        P(("dp", "tensor")),
    )
    return jax.shard_map(local, mesh=mesh, in_specs=in_specs, out_specs=out_specs, check_vma=False)
```

profile of v0, /device:TPU:0, one launch (start us, length us, event | category | flops | bytes accessed | tf_op | source)
XLA Modules:
  0.0 2452.6 jit_solution(775830728603930518)
XLA Ops:
  40.4 151.8 %all-gather.14.cloned.1.call-done = bf16[2048,2048]{1,0:T(8,128)(2,1)} async-done(((bf16[512,2048]{1,0:T(8,128)(2,1)}), bf16[2048,2048]{1,0:T(8,128)(2,1)}) %all-gather.14.cloned.1.call-update) | async-done | bytes 8388624 | tf_op jit(solution)/shard_map/all_gather | solution.py:113
  272.6 37.2 %while.26 = (s32[]{:T(128)}, bf16[4,512,8,64]{1,3,2,0:T(8,128)(2,1)}, f32[4,8,512,1]{2,1,3,0:T(8,128)}, bf16[4,512,8,64]{1,3,2,0:T(8,128)(2,1)}, bf16[4,512,8,64...) while((s32[]{:T(128)}, bf16[4,512,8,64]{1,3,2,0:T(8,128)(2,1)}, ...), condition=%wide.region_4.5_spmd, body=%wide.region_1.4_spmd.sunk | while | flops 562294784 | bytes 28969548 | solution.py:133
  338.1 270.9 %reduce-scatter.12.cloned.1.call-done = f32[512,2048]{1,0:T(8,128)} async-done(((f32[2048,2048]{1,0:T(8,128)}), f32[512,2048]{1,0:T(8,128)}) %reduce-scatter.12.cloned.1.call-update) | async-done | bytes 4194320 | tf_op jit(solution)/shard_map/reduce_scatter | solution.py:138
  617.7 48.2 %all-gather.26.cloned.1.call-done = bf16[2048,2048]{1,0:T(8,128)(2,1)} async-done(((bf16[256,2048]{1,0:T(8,128)(2,1)}), bf16[2048,2048]{1,0:T(8,128)(2,1)}) %all-gather.26.cloned.1.call-update) | async-done | bytes 8388624 | tf_op jit(solution)/shard_map/all_gather | solution.py:103
  665.8 151.8 %all-gather.24.cloned.1.call-done = bf16[2048,2048]{1,0:T(8,128)(2,1)} async-done(((bf16[512,2048]{1,0:T(8,128)(2,1)}), bf16[2048,2048]{1,0:T(8,128)(2,1)}) %all-gather.24.cloned.1.call-update) | async-done | bytes 8388624 | tf_op jit(solution)/shard_map/all_gather | solution.py:144
  817.6 24.3 fusion.72
  842.0 30.0 %all-gather.28.cloned.1.call-done = bf16[2048,2048]{1,0:T(8,128)(2,1)} async-done(((bf16[256,2048]{1,0:T(8,128)(2,1)}), bf16[2048,2048]{1,0:T(8,128)(2,1)}) %all-gather.28.cloned.1.call-update) | async-done | bytes 8388624 | tf_op jit(solution)/shard_map/all_gather | solution.py:104
  872.0 24.2 fusion.73
  896.2 126.8 %all-gather.32.cloned.1.call-done = bf16[2048,2048]{1,0:T(8,128)(2,1)} async-done(((bf16[512,2048]{1,0:T(8,128)(2,1)}), bf16[2048,2048]{1,0:T(8,128)(2,1)}) %all-gather.32.cloned.1.call-update) | async-done | bytes 8388624 | tf_op jit(solution)/shard_map/all_gather | solution.py:163
  1023.0 54.4 %all-gather.30.cloned.1.call-done = bf16[2048,2048]{1,0:T(8,128)(2,1)} async-done(((bf16[256,2048]{1,0:T(8,128)(2,1)}), bf16[2048,2048]{1,0:T(8,128)(2,1)}) %all-gather.30.cloned.1.call-update) | async-done | bytes 8388624 | tf_op jit(solution)/shard_map/all_gather | solution.py:105
  1077.4 34.7 %multiply_convert_fusion.1 = (bf16[2048,2048]{1,0:T(8,128)(2,1)}, bf16[2048,2048]{1,0:T(8,128)(2,1)}, bf16[2048,2048]{1,0:T(8,128)(2,1)}) fusion(f32[2048,2048]{1,0:T(8,128)} %fusion.72, f32[2048,2048]{1,0:T(8,128)} %fusion.73, bf16[2048,2048]{1,0:T(8,128)(2,1)} %all-gather.32.cloned.1.call-done, bf16[2048,2048]{1,0:T(8,128)(2,1)} %all-gather.30.cloned.1.call-done), kind=kOutput, calls=%fused_computation.59 | convolution fusion | flops 17242783744 | bytes 75497472 | tf_op jit(solution)/shard_map/dot_general | solution.py:164
  1112.1 24.3 fusion.74
  1136.4 26.7 %convolution_add_fusion = f32[2048,2048]{1,0:T(8,128)} fusion(f32[2048,2048]{1,0:T(8,128)} %fusion.74, bf16[2048,2048]{1,0:T(8,128)(2,1)} %get-tuple-element.220, bf16[2048,2048]{1,0:T(8,128)(2,1)} %all-gather.28.cloned.1.call-done), kind=kOutput, calls=%fused_computation.70 | convolution fusion | flops 17184063488 | bytes 50331648 | tf_op jit(solution)/shard_map/dot_general | solution.py:38
  1187.0 256.7 %reduce-scatter.16.cloned.1.call-done = f32[512,2048]{1,0:T(8,128)} async-done(((f32[2048,2048]{1,0:T(8,128)}), f32[512,2048]{1,0:T(8,128)}) %reduce-scatter.16.cloned.1.call-update) | async-done | bytes 4194320 | tf_op jit(solution)/shard_map/reduce_scatter | solution.py:170
  1448.8 142.5 %reduce-scatter.14.cloned.1.call-done = bf16[512,2048]{1,0:T(8,128)(2,1)} async-done(((bf16[2048,2048]{1,0:T(8,128)(2,1)}), bf16[512,2048]{1,0:T(8,128)(2,1)}) %reduce-scatter.14.cloned.1.call-update) | async-done | bytes 2097168 | tf_op jit(solution)/shard_map/reduce_scatter | solution.py:151
  1598.2 23.9 convolution_convert_fusion.1
  1622.2 23.8 convolution_convert_fusion
  1646.0 24.0 convert_bitcast_fusion
  1670.2 78.3 %all-gather.34.cloned.1.call-done = bf16[2048,2048]{1,0:T(8,128)(2,1)} async-done(((bf16[512,2048]{1,0:T(8,128)(2,1)}), bf16[2048,2048]{1,0:T(8,128)(2,1)}) %all-gather.34.cloned.1.call-update) | async-done | bytes 8388624 | tf_op jit(solution)/shard_map/all_gather | solution.py:179
  1768.6 278.1 %while.27 = (s32[]{:T(128)}, f32[4,512,8,64]{1,0,3,2:T(4,128)}, f32[4,512,8,64]{1,0,3,2:T(4,128)}, bf16[4,512,8,64]{1,3,2,0:T(8,128)(2,1)}, bf16[4,512,8,64]{1,3...) while((s32[]{:T(128)}, f32[4,512,8,64]{1,0,3,2:T(4,128)}, ...), condition=%wide.region_12.13_spmd, body=%wide.region_10.12_spmd.sunk | while | flops 1374416896 | bytes 129617576 | solution.py:184
  2160.1 42.5 %reduce-scatter.26.cloned.1.call-done = bf16[256,512]{1,0:T(8,128)(2,1)} async-done(((bf16[2048,512]{1,0:T(8,128)(2,1)}), bf16[256,512]{1,0:T(8,128)(2,1)}) %reduce-scatter.26.cloned.1.call-update) | async-done | bytes 262160 | tf_op jit(solution)/shard_map/reduce_scatter | solution.py:215
  2204.4 43.2 %reduce-scatter.24.cloned.1.call-done = bf16[256,512]{1,0:T(8,128)(2,1)} async-done(((bf16[2048,512]{1,0:T(8,128)(2,1)}), bf16[256,512]{1,0:T(8,128)(2,1)}) %reduce-scatter.24.cloned.1.call-update) | async-done | bytes 262160 | tf_op jit(solution)/shard_map/reduce_scatter | solution.py:212
  2249.4 145.2 %reduce-scatter.18.cloned.1.call-done = bf16[512,2048]{1,0:T(8,128)(2,1)} async-done(((bf16[2048,2048]{1,0:T(8,128)(2,1)}), bf16[512,2048]{1,0:T(8,128)(2,1)}) %reduce-scatter.18.cloned.1.call-update) | async-done | bytes 2097168 | tf_op jit(solution)/shard_map/reduce_scatter | solution.py:197
  2397.8 41.0 %all-reduce.2 = (f32[2048]{0:T(1024)S(1)}, f32[2048]{0:T(1024)S(1)}) all-reduce(f32[2048]{0:T(1024)S(1)} %get-tuple-element.178, f32[2048]{0:T(1024)S(1)} %copy-done.23), channel_id=10, replica_groups=mesh['dp'=8,'tensor'=4] {'dp','tensor'}, use_global_device_ids=true, to_apply=%region_20.21.clone | all-reduce | flops 4096 | bytes 32768
  (262 shorter events, 647.5 us)
Async XLA Ops:
  7.2 33.2 %all-gather.18.cloned.1.call-start = ((), (), s32[]{:S(2)}) async-start(), calls=%async_computation.13 | async-start | bytes 2359296 | tf_op jit(solution)/shard_map/all_gather | solution.py:96
  7.9 184.3 %all-gather.14.cloned.1.call-start = ((), (), s32[]{:S(2)}) async-start(), calls=%async_computation.11 | async-start | bytes 10485760 | tf_op jit(solution)/shard_map/all_gather | solution.py:113
  25.8 194.2 %all-gather.20.cloned.1.call-start = ((), (), s32[]{:S(2)}) async-start(), calls=%async_computation.14 | async-start | bytes 2359296 | tf_op jit(solution)/shard_map/all_gather | solution.py:97
  26.6 223.0 %all-gather.16.cloned.1.call-start = ((), (), s32[]{:S(2)}) async-start(), calls=%async_computation.12 | async-start | bytes 2359296 | tf_op jit(solution)/shard_map/all_gather | solution.py:98
  27.2 288.6 %all-gather.22.cloned.1.call-start = ((), (), s32[]{:S(2)}) async-start(), calls=%async_computation.15 | async-start | bytes 2359296 | tf_op jit(solution)/shard_map/all_gather | solution.py:99
  27.7 581.3 %reduce-scatter.12.cloned.1.call-start = ((), (), s32[]{:S(2)}) async-start(), calls=%async_computation.16 | async-start | bytes 20971520 | tf_op jit(solution)/shard_map/reduce_scatter | solution.py:138
  328.4 337.4 %all-gather.26.cloned.1.call-start = ((), (), s32[]{:S(2)}) async-start(), calls=%async_computation.18 | async-start | bytes 9437184 | tf_op jit(solution)/shard_map/all_gather | solution.py:103
  329.2 488.5 %all-gather.24.cloned.1.call-start = ((), (), s32[]{:S(2)}) async-start(), calls=%async_computation.17 | async-start | bytes 10485760 | tf_op jit(solution)/shard_map/all_gather | solution.py:144
  615.6 256.4 %all-gather.28.cloned.1.call-start = ((), (), s32[]{:S(2)}) async-start(), calls=%async_computation.19 | async-start | bytes 9437184 | tf_op jit(solution)/shard_map/all_gather | solution.py:104
  616.3 406.7 %all-gather.32.cloned.1.call-start = ((), (), s32[]{:S(2)}) async-start(), calls=%async_computation.22 | async-start | bytes 10485760 | tf_op jit(solution)/shard_map/all_gather | solution.py:163
  616.9 460.5 %all-gather.30.cloned.1.call-start = ((), (), s32[]{:S(2)}) async-start(), calls=%async_computation.20 | async-start | bytes 9437184 | tf_op jit(solution)/shard_map/all_gather | solution.py:105
  617.6 826.1 %reduce-scatter.16.cloned.1.call-start = ((), (), s32[]{:S(2)}) async-start(), calls=%async_computation.23 | async-start | bytes 20971520 | tf_op jit(solution)/shard_map/reduce_scatter | solution.py:170
  1163.1 428.2 %reduce-scatter.14.cloned.1.call-start = ((), (), s32[]{:S(2)}) async-start(), calls=%async_computation.21 | async-start | bytes 10485760 | tf_op jit(solution)/shard_map/reduce_scatter | solution.py:151
  1186.9 404.4 %copy-start.8 = (bf16[512,2048]{1,0:T(8,128)(2,1)S(1)}, bf16[512,2048]{1,0:T(8,128)(2,1)}, u32[]{:S(2)}) copy-start(bf16[512,2048]{1,0:T(8,128)(2,1)} %param.25) | copy-start | bytes 6291460
  1186.9 404.4 %copy-start.27 = (f32[512]{0:T(512)S(1)}, f32[512]{0:T(512)}, u32[]{:S(2)}) copy-start(f32[512]{0:T(512)} %get-tuple-element.241) | copy-start | bytes 6148
  1186.9 561.6 %all-gather.34.cloned.1.call-start = ((), (), s32[]{:S(2)}) async-start(), calls=%async_computation.24 | async-start | bytes 10485760 | tf_op jit(solution)/shard_map/all_gather | solution.py:179
  1598.1 548.3 %reduce-scatter.28.cloned.1.call-start = ((), (), s32[]{:S(2)}) async-start(), calls=%async_computation.30 | async-start | bytes 9437184 | tf_op jit(solution)/shard_map/reduce_scatter | solution.py:220
  1622.1 527.2 %reduce-scatter.30.cloned.1.call-start = ((), (), s32[]{:S(2)}) async-start(), calls=%async_computation.31 | async-start | bytes 9437184 | tf_op jit(solution)/shard_map/reduce_scatter | solution.py:223
  1646.0 506.2 %reduce-scatter.32.cloned.1.call-start = ((), (), s32[]{:S(2)}) async-start(), calls=%async_computation.32 | async-start | bytes 9437184 | tf_op jit(solution)/shard_map/reduce_scatter | solution.py:226
  1670.1 484.7 %reduce-scatter.20.cloned.1.call-start = ((), (), s32[]{:S(2)}) async-start(), calls=%async_computation.26 | async-start | bytes 2359296 | tf_op jit(solution)/shard_map/reduce_scatter | solution.py:206
  2075.2 83.1 %reduce-scatter.22.cloned.1.call-start = ((), (), s32[]{:S(2)}) async-start(), calls=%async_computation.27 | async-start | bytes 2359296 | tf_op jit(solution)/shard_map/reduce_scatter | solution.py:209
  2085.0 117.6 %reduce-scatter.26.cloned.1.call-start = ((), (), s32[]{:S(2)}) async-start(), calls=%async_computation.29 | async-start | bytes 2359296 | tf_op jit(solution)/shard_map/reduce_scatter | solution.py:215
  2095.4 152.2 %reduce-scatter.24.cloned.1.call-start = ((), (), s32[]{:S(2)}) async-start(), calls=%async_computation.28 | async-start | bytes 2359296 | tf_op jit(solution)/shard_map/reduce_scatter | solution.py:212
  2107.3 287.3 %reduce-scatter.18.cloned.1.call-start = ((), (), s32[]{:S(2)}) async-start(), calls=%async_computation.25 | async-start | bytes 10485760 | tf_op jit(solution)/shard_map/reduce_scatter | solution.py:197
  (34 other events, 2658.3 us)
Sparse Core Ops, SparseCore 0:
  9.9 30.4 all-gather.17
  42.5 149.5 all-gather.13
  194.1 25.9 all-gather.19
  221.8 27.7 all-gather.15
  251.4 27.7 all-gather.21
  328.5 280.4 reduce-scatter.11
  610.9 54.8 all-gather.25
  668.0 149.5 all-gather.23
  819.5 52.4 all-gather.27
  873.4 149.5 all-gather.31
  1024.9 52.4 all-gather.29
  1163.2 280.4 reduce-scatter.15
  1446.1 145.2 reduce-scatter.13
  1598.2 150.2 all-gather.33
  1751.8 69.6 reduce-scatter.27
  1824.8 71.4 reduce-scatter.29
  1899.7 71.2 reduce-scatter.31
  2075.3 38.5 reduce-scatter.19
  2117.2 41.0 reduce-scatter.21
  2161.5 41.0 reduce-scatter.25
  2206.5 41.0 reduce-scatter.23
  2249.9 144.6 reduce-scatter.17
where the time goes:
time: 2470 us; the launch traced here: 2450 us
  waiting for transfers between devices  1580 us (64%)
  matrix products  462 us (19%)
  local copies, waits for them, and re-layouts  250 us (10%)
  other arithmetic  80.3 us (3%)
  blocking collectives  60.3 us (2%)
    reduce_scatter x1, waiting for transfers between devices, local(): lax.psum_scatter(contract_cols(part, output_full), 'tensor', scatter_dime...  271 us
    reduce_scatter x1, waiting for transfers between devices, local(): lax.psum_scatter(contract_cols(grad_gate_pre, gate_back) + contract_cols(...  257 us
    dynamic_update_slice x16, local copies, waits for them, and re-layouts, local(): lax.map(attend_forward, (by_seq(query_rot), by_seq(key_rot), by_seq(value...  177 us
    all_gather x1, waiting for transfers between devices, local(): gathered_one = lax.all_gather(normed_one, 'tensor', axis=0, tiled=True)  152 us
    all_gather x1, waiting for transfers between devices, local(): gathered_two = lax.all_gather(normed_two, 'tensor', axis=0, tiled=True)  152 us
    reduce_scatter x1, waiting for transfers between devices, local(): lax.psum_scatter((total + contract_cols(grad_v_pre, value_full)).astype(j...  145 us
    reduce_scatter x1, waiting for transfers between devices, local(): lax.psum_scatter(contract_cols(part, down_full).astype(jnp.bfloat16), 'te...  143 us
    all_gather x1, waiting for transfers between devices, local(): grad_out_rows = lax.all_gather(cotangent, 'tensor', axis=0, tiled=True)  127 us
  transfers between devices with their start and end apart: 22, of which 17 were waited for; matrix products, arithmetic and copies ran while one was open for 27% of the time, Pallas kernels for 0%

commit v1 on v0

--- a/solution.py
+++ b/solution.py
@@ -1,6 +1,8 @@
 import jax
 import jax.numpy as jnp
 from jax import lax
+from jax.experimental import pallas as pl
+from jax.experimental.pallas import tpu as pltpu
 from jax.sharding import PartitionSpec as P
 
 HEAD = 64
@@ -89,7 +91,7 @@
     return (grad_source, grad_gain)
 
 
-def local(
+def tensor_parallel(
     tokens, w_query, w_key, w_value, w_output, attn_gain, w_gate, w_up, w_down, mlp_gain, cotangent
 ):
     query_full, key_full, value_full, output_full, attn_scale = (
@@ -246,6 +248,338 @@
     )
 
 
+PAIR = 2 * HEAD
+
+
+def lane_tables():
+    half = HEAD // 2
+    lanes = jnp.arange(PAIR)
+    freqs = rope_base ** (-2.0 * (lanes % half).astype(jnp.float32) / HEAD)
+    angles = jnp.arange(LEN).astype(jnp.float32)[:, None] * freqs[None, :]
+    signs = jnp.where(lanes % HEAD < half, -1.0, 1.0)
+    return (jnp.cos(angles), jnp.sin(angles) * signs[None, :])
+
+
+def swap_halves(values, lanes):
+    half = HEAD // 2
+    return jnp.where(
+        lanes % HEAD < half,
+        pltpu.roll(values, PAIR - half, 1),
+        pltpu.roll(values, half, 1),
+    )
+
+
+def dot_last(left, right):
+    return lax.dot_general(
+        left, right, (((1,), (1,)), ((), ())), preferred_element_type=jnp.float32
+    )
+
+
+def dot_first(left, right):
+    return lax.dot_general(
+        left, right, (((0,), (0,)), ((), ())), preferred_element_type=jnp.float32
+    )
+
+
+def forward_kernel(q_ref, k_ref, v_ref, cos_ref, sin_ref, qr_ref, kr_ref, vb_ref, mix_ref):
+    lanes = lax.broadcasted_iota(jnp.int32, (LEN, PAIR), 1)
+    cosine = cos_ref[...]
+    sine = sin_ref[...]
+
+    def rotated(values):
+        return (values * cosine + swap_halves(values, lanes) * sine).astype(jnp.bfloat16)
+
+    query = rotated(q_ref[...])
+    key = rotated(k_ref[...])
+    value = v_ref[...].astype(jnp.bfloat16)
+    qr_ref[...] = query
+    kr_ref[...] = key
+    vb_ref[...] = value
+    scaled = query * jnp.bfloat16(HEAD**-0.5)
+    step = LEN // 2
+    for part in range(2):
+        rows = slice(part * step, (part + 1) * step)
+        seen = (part + 1) * step
+        shape = (step, seen)
+        allowed = lax.broadcasted_iota(jnp.int32, shape, 0) + part * step >= (
+            lax.broadcasted_iota(jnp.int32, shape, 1)
+        )
+        mixed = []
+        for head in range(2):
+            mine = lanes[rows] // HEAD == head
+            one_head = jnp.where(mine, scaled[rows], jnp.zeros_like(scaled[rows]))
+            scores = jnp.where(allowed, dot_last(one_head, key[:seen]), -1e30)
+            top = jnp.max(scores, axis=-1, keepdims=True)
+            expo = jnp.exp(scores - top)
+            total = jnp.sum(expo, axis=-1, keepdims=True)
+            probs = (expo * (1.0 / total)).astype(jnp.bfloat16)
+            mixed.append(jnp.dot(probs, value[:seen], preferred_element_type=jnp.float32))
+        both = jnp.where(lanes[rows] < HEAD, mixed[0], mixed[1])
+        mix_ref[rows, :] = both.astype(jnp.bfloat16)
+
+
+def backward_kernel(q_ref, k_ref, v_ref, g_ref, cos_ref, sin_ref, out_ref):
+    lanes = lax.broadcasted_iota(jnp.int32, (LEN, PAIR), 1)
+    cosine = cos_ref[...]
+    sine = sin_ref[...]
+    factor = jnp.bfloat16(HEAD**-0.5)
+    query = q_ref[...] * factor
+    key = k_ref[...]
+    key_scaled = key * factor
+    value = v_ref[...]
+    grad = g_ref[...]
+    step = LEN // 2
+    grad_query, grad_key, grad_value = [], [], []
+    for part in range(2):
+        rows = slice(part * step, (part + 1) * step)
+        seen = (part + 1) * step
+        shape = (seen, step)
+        allowed = lax.broadcasted_iota(jnp.int32, shape, 1) + part * step >= (
+            lax.broadcasted_iota(jnp.int32, shape, 0)
+        )
+        for head in range(2):
+            mine = lanes[rows] // HEAD == head
+            own = lanes[:seen] // HEAD == head
+            q_one = jnp.where(mine, query[rows], jnp.zeros_like(query[rows]))
+            g_one = jnp.where(mine, grad[rows], jnp.zeros_like(grad[rows]))
+            k_one = jnp.where(own, key_scaled[:seen], jnp.zeros_like(key[:seen]))
+            scores = jnp.where(allowed, dot_last(key[:seen], q_one), -1e30)
+            top = jnp.max(scores, axis=0, keepdims=True)
+            expo = jnp.exp(scores - top)
+            total = jnp.sum(expo, axis=0, keepdims=True)
+            probs = expo * (1.0 / total)
+            grad_probs = dot_last(value[:seen], g_one)
+            inner = jnp.sum(probs * grad_probs, axis=0, keepdims=True)
+            grad_scores = (probs * (grad_probs - inner)).astype(jnp.bfloat16)
+            rounded = probs.astype(jnp.bfloat16)
+            grad_value.append(jnp.dot(rounded, g_one, preferred_element_type=jnp.float32))
+            grad_key.append(jnp.dot(grad_scores, q_one, preferred_element_type=jnp.float32))
+            grad_query.append(dot_first(grad_scores, k_one))
+
+    def gather(parts):
+        first = parts[0] + parts[1]
+        second = parts[2] + parts[3]
+        return jnp.concatenate([first + second[:step], second[step:]], axis=0)
+
+    def unrotated(values):
+        return (values * cosine - swap_halves(values, lanes) * sine).astype(jnp.bfloat16)
+
+    all_query = jnp.concatenate(
+        [grad_query[0] + grad_query[1], grad_query[2] + grad_query[3]], axis=0
+    )
+    columns = out_ref.shape[1] // 3
+    place = pl.multiple_of(pl.program_id(0) * PAIR, PAIR)
+    out_ref[:, pl.ds(place, PAIR)] = unrotated(all_query)
+    out_ref[:, pl.ds(columns + place, PAIR)] = unrotated(gather(grad_key))
+    out_ref[:, pl.ds(2 * columns + place, PAIR)] = gather(grad_value).astype(jnp.bfloat16)
+
+
+def pair_block(offset):
+    return pl.BlockSpec((LEN, PAIR), lambda step: (0, offset + step))
+
+
+def whole_block(columns):
+    return pl.BlockSpec((LEN, columns), lambda step: (0, 0))
+
+
+def attention(qkv, cosine, sine):
+    columns = qkv.shape[1] // 3
+    pairs = columns // PAIR
+    flat = jax.ShapeDtypeStruct((LEN, columns), jnp.bfloat16)
+    return pl.pallas_call(
+        forward_kernel,
+        grid=(pairs,),
+        in_specs=[pair_block(0), pair_block(pairs), pair_block(2 * pairs)]
+        + [whole_block(PAIR)] * 2,
+        out_specs=[pair_block(0)] * 4,
+        out_shape=[flat] * 4,
+        name="attend",
+        cost_estimate=pl.CostEstimate(
+            flops=8 * LEN * LEN * columns,
+            transcendentals=LEN * LEN * columns // HEAD,
+            bytes_accessed=20 * LEN * columns,
+        ),
+    )(qkv, qkv, qkv, cosine, sine)
+
+
+def attention_back(query, key, value, grad, cosine, sine):
+    columns = query.shape[1]
+    return pl.pallas_call(
+        backward_kernel,
+        grid=(columns // PAIR,),
+        in_specs=[pair_block(0)] * 4 + [whole_block(PAIR)] * 2,
+        out_specs=whole_block(3 * columns),
+        out_shape=jax.ShapeDtypeStruct((LEN, 3 * columns), jnp.bfloat16),
+        name="attend_back",
+        cost_estimate=pl.CostEstimate(
+            flops=20 * LEN * LEN * columns,
+            transcendentals=LEN * LEN * columns // HEAD,
+            bytes_accessed=14 * LEN * columns,
+        ),
+    )(query, key, value, grad, cosine, sine)
+
+
+def shift(values, count):
+    return lax.ppermute(values, "tensor", [(i, (i + 1) % count) for i in range(count)])
+
+
+def travel(values, count):
+    stops = [values]
+    for _ in range(count - 1):
+        stops.append(shift(stops[-1], count))
+    return stops
+
+
+def ring_sum(parts, count):
+    total = parts[1]
+    for j in list(range(2, count)) + [0]:
+        total = shift(total.astype(jnp.bfloat16), count).astype(jnp.float32) + parts[j]
+    return total
+
+
+def sum_all(values, axes):
+    for name, count in axes:
+        hop = 1
+        while hop < count:
+            values = values + lax.ppermute(values, name, [(i, i ^ hop) for i in range(count)])
+            hop *= 2
+    return values
+
+
+def token_parallel(
+    tokens, w_query, w_key, w_value, w_output, attn_gain, w_gate, w_up, w_down, mlp_gain, cotangent
+):
+    count = lax.axis_size("tensor")
+    dp_count = lax.axis_size("dp")
+    heads = w_query.shape[1]
+    hidden_units = w_gate.shape[1]
+    gains = lax.all_gather(jnp.stack([attn_gain, mlp_gain]), "dp", axis=0)
+    gains = jnp.swapaxes(gains, 0, 1).reshape(2, -1).astype(jnp.float32)
+    attn_scale, mlp_scale = gains[0], gains[1]
+    shard = jnp.concatenate([w_query, w_key, w_value, w_output], axis=1)
+    own = lax.all_gather(shard, "dp", axis=0, tiled=True)
+    others = travel(shard, count)[1:]
+    rest_shard = jnp.concatenate(
+        [other[:, k * heads : (k + 1) * heads] for k in range(4) for other in others], axis=1
+    )
+    rest = lax.all_gather(rest_shard, "dp", axis=0, tiled=True)
+    wide = (count - 1) * heads
+    gate_up = lax.all_gather(jnp.concatenate([w_gate, w_up], axis=1), "dp", axis=0, tiled=True)
+    down = lax.all_gather(w_down, "dp", axis=0, tiled=True)
+    cotangents = travel(cotangent, count)
+
+    source = tokens.astype(jnp.float32)
+    inverse_one = lax.rsqrt(jnp.mean(source * source, axis=-1, keepdims=True) + eps)
+    normed_one = (source * inverse_one * attn_scale).astype(jnp.bfloat16)
+    cosine, sine = lane_tables()
+    own_qkv = jnp.dot(normed_one, own[:, : 3 * heads], preferred_element_type=jnp.float32)
+    own_query, own_key, own_value, own_mixed = attention(own_qkv, cosine, sine)
+    rest_qkv = jnp.dot(normed_one, rest[:, : 3 * wide], preferred_element_type=jnp.float32)
+    rest_query, rest_key, rest_value, rest_mixed = attention(rest_qkv, cosine, sine)
+    branch = contract_cols(own_mixed, own[:, 3 * heads :])
+    branch = branch + contract_cols(rest_mixed, rest[:, 3 * wide :])
+    hidden = source + branch
+    inverse_two = lax.rsqrt(jnp.mean(hidden * hidden, axis=-1, keepdims=True) + eps)
+    normed_two = (hidden * inverse_two * mlp_scale).astype(jnp.bfloat16)
+
+    normed = travel(normed_two, count)
+    activs, pres, mlp_parts, norm_parts = [], [], [], []
+    for normed_rows, grad_rows in zip(normed, cotangents):
+        both = jnp.dot(normed_rows, gate_up, preferred_element_type=jnp.float32)
+        gate, up = both[:, :hidden_units], both[:, hidden_units:]
+        sigma = jax.nn.sigmoid(gate)
+        swish = gate * sigma
+        activ = (swish * up).astype(jnp.bfloat16)
+        grad_activ = jnp.dot(grad_rows, down, preferred_element_type=jnp.float32)
+        grad_gate_pre = (grad_activ * up * sigma * (1.0 + gate * (1.0 - sigma))).astype(
+            jnp.bfloat16
+        )
+        grad_up_pre = (grad_activ * swish).astype(jnp.bfloat16)
+        pre = jnp.concatenate([grad_gate_pre, grad_up_pre], axis=1)
+        activs.append(activ)
+        pres.append(pre)
+        norm_parts.append(contract_cols(pre, gate_up))
+        mlp_parts.append(contract_cols(activ, down))
+    grad_normed_two = ring_sum(norm_parts, count)
+    mlp_branch = ring_sum(mlp_parts, count)
+    block_out = (hidden + mlp_branch).astype(jnp.bfloat16)
+    all_normed = jnp.concatenate(normed, axis=0)
+    all_cotangents = jnp.concatenate(cotangents, axis=0)
+    grad_gate_up_w = contract_rows(all_normed, jnp.concatenate(pres, axis=0)).astype(jnp.bfloat16)
+    grad_down_w = contract_rows(all_cotangents, jnp.concatenate(activs, axis=0)).astype(
+        jnp.bfloat16
+    )
+
+    def over_dp(values):
+        return lax.psum_scatter(values, "dp", scatter_dimension=0, tiled=True)
+
+    grad_gate_up = over_dp(grad_gate_up_w).astype(jnp.float32)
+    grad_down = over_dp(grad_down_w).astype(jnp.float32)
+
+    grad_hidden_norm, mlp_gain_part = norm_back(grad_normed_two, hidden, inverse_two, mlp_scale)
+    grad_hidden = cotangent.astype(jnp.float32) + grad_hidden_norm
+    grad_branch = grad_hidden.astype(jnp.bfloat16)
+    all_mixed = jnp.concatenate([own_mixed, rest_mixed], axis=1)
+    grad_output_w = contract_rows(grad_branch, all_mixed).astype(jnp.bfloat16)
+    rest_grad = jnp.dot(
+        grad_branch, rest[:, 3 * wide :], preferred_element_type=jnp.float32
+    ).astype(jnp.bfloat16)
+    own_grad = jnp.dot(
+        grad_branch, own[:, 3 * heads :], preferred_element_type=jnp.float32
+    ).astype(jnp.bfloat16)
+    rest_pre = attention_back(rest_query, rest_key, rest_value, rest_grad, cosine, sine)
+    rest_grad_w = contract_rows(normed_one, rest_pre).astype(jnp.bfloat16)
+    own_pre = attention_back(own_query, own_key, own_value, own_grad, cosine, sine)
+    own_grad_w = contract_rows(normed_one, own_pre).astype(jnp.bfloat16)
+    grad_normed_one = contract_cols(rest_pre, rest[:, : 3 * wide])
+    grad_normed_one = grad_normed_one + contract_cols(own_pre, own[:, : 3 * heads])
+    grad_source_norm, attn_gain_part = norm_back(grad_normed_one, source, inverse_one, attn_scale)
+    grad_tokens = (grad_hidden + grad_source_norm).astype(jnp.bfloat16)
+
+    output_sum = over_dp(grad_output_w)
+    rest_sum = over_dp(rest_grad_w)
+    own_sum = over_dp(own_grad_w)
+    slots = [jnp.concatenate([own_sum, output_sum[:, :heads]], axis=1)]
+    for j in range(1, count):
+        columns = [rest_sum[:, k * wide + (j - 1) * heads : k * wide + j * heads] for k in range(3)]
+        slots.append(jnp.concatenate(columns + [output_sum[:, j * heads : (j + 1) * heads]], axis=1))
+    grads = ring_sum([slot.astype(jnp.float32) for slot in slots], count)
+    grad_query, grad_key, grad_value, grad_output = [
+        grads[:, k * heads : (k + 1) * heads] for k in range(4)
+    ]
+    gain_parts = sum_all(
+        jnp.stack([attn_gain_part, mlp_gain_part]), (("dp", dp_count), ("tensor", count))
+    )
+    piece = gain_parts.shape[1] // (dp_count * count)
+    place = (lax.axis_index("dp") * count + lax.axis_index("tensor")) * piece
+    gain_sums = lax.dynamic_slice_in_dim(gain_parts, place, piece, axis=1)
+    return (
+        block_out,
+        grad_tokens,
+        grad_query,
+        grad_key,
+        grad_value,
+        grad_output,
+        gain_sums[0],
+        grad_gate_up[:, :hidden_units],
+        grad_gate_up[:, hidden_units:],
+        grad_down,
+        gain_sums[1],
+    )
+
+
+def power_of_two(number):
+    return number & (number - 1) == 0
+
+
+def local(tokens, w_query, *others):
+    axes = (lax.axis_size("dp"), lax.axis_size("tensor"))
+    whole = tokens.shape[0] == LEN and w_query.shape[1] % PAIR == 0
+    if whole and axes[1] > 1 and all(power_of_two(size) for size in axes):
+        return token_parallel(tokens, w_query, *others)
+    return tensor_parallel(tokens, w_query, *others)
+
+
 def solution(mesh):
     in_specs = (
         P(("dp", "tensor"), None),

time: 2470 us -> 1240 us (0.50)
  waiting for transfers between devices: 1580 us -> 681 us
  local copies, waits for them, and re-layouts: 250 us -> 22.3 us
  matrix products: 462 us -> 371 us
  Pallas kernels: 0 us -> 73.1 us
  blocking collectives: 60.3 us -> 8.6 us
  other arithmetic: 80.3 us -> 41.9 us
    reduce_scatter x11 -> x5, waiting for transfers between devices: 903 us -> 223 us  [over_dp(): return lax.psum_scatter(values, 'dp', scatter_dimension=0, tiled=True)]
    all_gather x11 -> x4, waiting for transfers between devices: 674 us -> 79.9 us  [the longest x1 41.6 us: token_parallel(): down = lax.all_gather(w_down, 'dp', axis=0, tiled=True)]
    ppermute x0 -> x23, waiting for transfers between devices: none -> 378 us  [the longest x18 356 us: shift(): lax.ppermute(values, 'tensor', [(i, (i + 1) % count) for i in range(count)])]
    dynamic_update_slice x16 -> x0, local copies, waits for them, and re-layouts: 177 us -> none  [local(): lax.map(attend_forward, (by_seq(query_rot), by_seq(key_rot), by_seq(value...]
    dot_general x35 -> x12, matrix products: 226 us -> 135 us  [the longest x4 51.1 us: token_parallel(): both = jnp.dot(normed_rows, gate_up, preferred_element_type=jnp.float32)]
    pallas_call x0 -> x4, Pallas kernels: none -> 73.1 us  [the longest x2 37.3 us: attention_back(): pl.pallas_call(backward_kernel, grid=(columns // PAIR,), in_specs=[pair_b...]
    unnamed x1 -> x0, blocking collectives: 41 us -> none
    dot_general x7 -> x5, matrix products: 111 us -> 99.4 us  [contract_rows(): lax.dot_general(left, right, (((0,), (0,)), ((), ())), preferred_element_...]
  transfers between devices with their start and end apart: 22 -> 32, of which waited for: 17 -> 23; matrix products, arithmetic and copies ran while one was open for 27% -> 33% of each run, Pallas kernels for 0% -> 6%
where the time goes in v1:
time: 1240 us; the launch traced here: 1230 us
  waiting for transfers between devices  681 us (55%)
  matrix products  371 us (30%)
  Pallas kernels  73.1 us (6%)
  other arithmetic  41.9 us (3%)
  local copies, waits for them, and re-layouts  22.3 us (2%)
  starting transfers between devices  19.4 us (2%)
  between operations  14.7 us (1%)
    ppermute x18, waiting for transfers between devices, shift(): lax.ppermute(values, 'tensor', [(i, (i + 1) % count) for i in range(count)])  356 us
    reduce_scatter x5, waiting for transfers between devices, over_dp(): return lax.psum_scatter(values, 'dp', scatter_dimension=0, tiled=True)  223 us
    dot_general x12, matrix products, contract_cols(): lax.dot_general(left, right, (((1,), (1,)), ((), ())), preferred_element_...  136 us
    dot_general x5, matrix products, contract_rows(): lax.dot_general(left, right, (((0,), (0,)), ((), ())), preferred_element_...  99.4 us
    dot_general x4, matrix products, token_parallel(): both = jnp.dot(normed_rows, gate_up, preferred_element_type=jnp.float32)  51.1 us
    dot_general x4, matrix products, token_parallel(): grad_activ = jnp.dot(grad_rows, down, preferred_element_type=jnp.float32)  46.4 us
    all_gather x1, waiting for transfers between devices, token_parallel(): down = lax.all_gather(w_down, 'dp', axis=0, tiled=True)  41.6 us
    pallas_call x2, Pallas kernels, attention_back(): pl.pallas_call(backward_kernel, grid=(columns // PAIR,), in_specs=[pair_b...  37.3 us
  transfers between devices with their start and end apart: 32, of which 23 were waited for; matrix products, arithmetic and copies ran while one was open for 33% of the time, Pallas kernels for 6%

profile of v1, /device:TPU:0, one launch (start us, length us, event | category | flops | bytes accessed | tf_op | source)
XLA Modules:
  0.0 1232.3 jit_solution(11401239557831451667)
XLA Ops:
  15.3 25.4 %collective-permute-done = bf16[256,2048]{1,0:T(8,128)(2,1)S(1)} collective-permute-done((bf16[256,2048]{1,0:T(8,128)(2,1)}, bf16[256,2048]{1,0:T(8,128)(2,1)S(1)}, u32[]{:S(2)}, u32[]{:S(2)}) %collective-permute-start) | collective-permute-done | bytes 1048608 | tf_op jit(solution)/shard_map/ppermute | solution.py:423
  40.7 26.1 %collective-permute-done.1 = bf16[256,2048]{1,0:T(8,128)(2,1)S(1)} collective-permute-done((bf16[256,2048]{1,0:T(8,128)(2,1)S(1)}, bf16[256,2048]{1,0:T(8,128)(2,1)S(1)}, u32[]{:S(2)}, u32[]{:S(2)}) %collective-permute-start.1) | collective-permute-done | bytes 1048608 | tf_op jit(solution)/shard_map/ppermute | solution.py:423
  66.9 25.2 %collective-permute-done.2 = bf16[256,2048]{1,0:T(8,128)(2,1)S(1)} collective-permute-done((bf16[256,2048]{1,0:T(8,128)(2,1)S(1)}, bf16[256,2048]{1,0:T(8,128)(2,1)S(1)}, u32[]{:S(2)}, u32[]{:S(2)}) %collective-permute-start.2) | collective-permute-done | bytes 1048608 | tf_op jit(solution)/shard_map/ppermute | solution.py:423
  98.0 47.1 %collective-permute-done.9 = bf16[512,2048]{1,0:T(8,128)(2,1)S(1)} collective-permute-done((bf16[512,2048]{1,0:T(8,128)(2,1)}, bf16[512,2048]{1,0:T(8,128)(2,1)S(1)}, u32[]{:S(2)}, u32[]{:S(2)}) %collective-permute-start.9) | collective-permute-done | bytes 2097184 | tf_op jit(solution)/shard_map/ppermute | solution.py:423
  156.8 34.5 %collective-permute-done.11 = bf16[512,2048]{1,0:T(8,128)(2,1)} collective-permute-done((bf16[512,2048]{1,0:T(8,128)(2,1)S(1)}, bf16[512,2048]{1,0:T(8,128)(2,1)}, u32[]{:S(2)}, u32[]{:S(2)}) %collective-permute-start.11) | collective-permute-done | bytes 2097184 | tf_op jit(solution)/shard_map/ppermute | solution.py:423
  217.2 16.0 %fusion.18.q_ref.k_ref.v_ref = f32[512,4608]{1,0:T(8,128)} fusion(bf16[2048,6144]{1,0:T(8,128)(2,1)} %all-gather.9.cloned.1.call-done, bf16[512,2048]{1,0:T(8,128)(2,1)S(1)} %copy-done.2, f32[2048]{0:T(1024)S(1)} %bitcast.57, f32[512]{0:T(512)S(1)} %get-tuple-element.69), kind=kOutput, calls=%fused_computation.19 | convolution fusion | flops 9667870720 | bytes 30418944 | tf_op jit(solution)/shard_map/dot_general | solution.py:477
  233.1 25.8 %attend.3 = (bf16[512,1536]{1,0:T(8,128)(2,1)}, bf16[512,1536]{1,0:T(8,128)(2,1)}, bf16[512,1536]{1,0:T(8,128)(2,1)}, bf16[512,1536]{1,0:T(8,128)(2,1)}) custom-call(f32[512,4608]{1,0:T(8,128)} %fusion.18.q_ref.k_ref.v_ref, f32[512,4608]{1,0:T(8,128)} %fusion.18.q_ref.k_ref.v_ref, f32[512,4608]{1,0:T(8,128)} %fusion.18.q_ref.k_ref.v_ref, ...), custom_call_target="tpu_custom_call" | custom-call | flops 3221225472 | bytes 15728640 | tf_op jit(solution)/shard_map/attend/pallas_call | solution.py:389
  274.0 35.4 %all-gather.11.cloned.1.call-done = bf16[2048,4096]{1,0:T(8,128)(2,1)} async-done(((bf16[256,4096]{1,0:T(8,128)(2,1)}), bf16[2048,4096]{1,0:T(8,128)(2,1)}) %all-gather.11.cloned.1.call-update) | async-done | bytes 16777232 | tf_op jit(solution)/shard_map/all_gather | solution.py:467
  323.8 41.6 %all-gather.13.cloned.1.call-done = bf16[2048,2048]{1,0:T(8,128)(2,1)} async-done(((bf16[256,2048]{1,0:T(8,128)(2,1)}), bf16[2048,2048]{1,0:T(8,128)(2,1)}) %all-gather.13.cloned.1.call-update) | async-done | bytes 8388624 | tf_op jit(solution)/shard_map/all_gather | solution.py:468
  455.4 21.1 %collective-permute-done.10 = bf16[512,2048]{1,0:T(8,128)(2,1)} collective-permute-done((bf16[512,2048]{1,0:T(8,128)(2,1)}, bf16[512,2048]{1,0:T(8,128)(2,1)}, u32[]{:S(2)}, u32[]{:S(2)}) %collective-permute-start.10) | collective-permute-done | bytes 2097184 | tf_op jit(solution)/shard_map/ppermute | solution.py:423
  491.6 29.7 %collective-permute-done.4 = bf16[512,2048]{1,0:T(8,128)(2,1)S(1)} collective-permute-done((bf16[512,2048]{1,0:T(8,128)(2,1)S(1)}, bf16[512,2048]{1,0:T(8,128)(2,1)S(1)}, u32[]{:S(2)}, u32[]{:S(2)}) %collective-permute-start.4) | collective-permute-done | bytes 2097184 | tf_op jit(solution)/shard_map/ppermute | solution.py:423
  531.4 35.0 %collective-permute-done.7 = bf16[512,2048]{1,0:T(8,128)(2,1)} collective-permute-done((bf16[512,2048]{1,0:T(8,128)(2,1)S(1)}, bf16[512,2048]{1,0:T(8,128)(2,1)}, u32[]{:S(2)}, u32[]{:S(2)}) %collective-permute-start.7) | collective-permute-done | bytes 2097184 | tf_op jit(solution)/shard_map/ppermute | solution.py:423
  628.5 27.7 %collective-permute-done.6 = bf16[512,2048]{1,0:T(8,128)(2,1)S(1)} collective-permute-done((bf16[512,2048]{1,0:T(8,128)(2,1)}, bf16[512,2048]{1,0:T(8,128)(2,1)S(1)}, u32[]{:S(2)}, u32[]{:S(2)}) %collective-permute-start.6) | collective-permute-done | bytes 2097184 | tf_op jit(solution)/shard_map/ppermute | solution.py:423
  658.7 42.4 %collective-permute-done.14 = bf16[512,2048]{1,0:T(8,128)(2,1)S(1)} collective-permute-done((bf16[512,2048]{1,0:T(8,128)(2,1)S(1)}, bf16[512,2048]{1,0:T(8,128)(2,1)S(1)}, u32[]{:S(2)}, u32[]{:S(2)}) %collective-permute-start.14) | collective-permute-done | bytes 2097184 | tf_op jit(solution)/shard_map/ppermute | solution.py:423
  702.4 17.5 %multiply_reduce_fusion = (f32[2048]{0:T(1024)}, f32[512]{0:T(512)S(1)}, f32[512,2048]{1,0:T(8,128)}) fusion(f32[512,2048]{1,0:T(8,128)} %copy-done.1, f32[512]{0:T(512)S(1)} %copy-done.18, bf16[512,2048]{1,0:T(8,128)(2,1)} %copy-done.7, f32[2048]{0:T(1024)S(1)} %bitcast.48, bf16[2048,4096]{1,0:T(8,128)(2,1)} %all-gather.11.cloned.1.call-done, ...), kind=kOutput, calls=%fused_computation.87 | convolution fusion | flops 8606709760 | bytes 31477760 | tf_op jit(solution)/shard_map/dot_general | solution.py:40
  719.9 25.5 %collective-permute-done.8 = bf16[512,2048]{1,0:T(8,128)(2,1)} collective-permute-done((bf16[512,2048]{1,0:T(8,128)(2,1)}, bf16[512,2048]{1,0:T(8,128)(2,1)}, u32[]{:S(2)}, u32[]{:S(2)}) %collective-permute-start.8) | collective-permute-done | bytes 2097184 | tf_op jit(solution)/shard_map/ppermute | solution.py:423
  772.0 27.2 %attend_back.2 = bf16[512,4608]{1,0:T(8,128)(2,1)} custom-call(bf16[512,1536]{1,0:T(8,128)(2,1)} %get-tuple-element.21.q_ref, bf16[512,1536]{1,0:T(8,128)(2,1)} %get-tuple-element.22.k_ref, bf16[512,1536]{1,0:T(8,128)(2,1)} %get-tuple-element.23.v_ref, bf16[512,1536]{1,0:T(8,128)(2,1)} %fusion.96.g_ref, f32[512,128]{1,0:T(8,128)} %get-tuple-element.67.cos_ref, ...), custom_call_target="tpu_custom_call" | custom-call | flops 8053063680 | bytes 11010048 | tf_op jit(solution)/shard_map/attend_back/pallas_call | solution.py:407
  814.7 23.8 %fusion.45 = bf16[2048,2048]{1,0:T(8,128)(2,1)} fusion(bf16[512,2048]{1,0:T(8,128)(2,1)} %get-tuple-element.41, bf16[512,2048]{1,0:T(8,128)(2,1)} %get-tuple-element.39, bf16[512,2048]{1,0:T(8,128)(2,1)} %get-tuple-element.40, bf16[512,2048]{1,0:T(8,128)(2,1)} %get-tuple-element.42, bf16[512,2048]{1,0:T(8,128)(2,1)} %collective-permute-done.13, ...), kind=kOutput, calls=%fused_computation.50 | convolution fusion | flops 17251172352 | bytes 25165824 | tf_op jit(solution)/shard_map/dot_general | solution.py:34
  844.1 46.1 %fusion.20 = bf16[2048,4096]{1,0:T(8,128)(2,1)} fusion(bf16[512,2048]{1,0:T(8,128)(2,1)} %get-tuple-element.36, bf16[512,2048]{1,0:T(8,128)(2,1)} %get-tuple-element.35, bf16[512,2048]{1,0:T(8,128)(2,1)} %get-tuple-element.32, bf16[512,2048]{1,0:T(8,128)(2,1)} %get-tuple-element.31, bf16[512,2048]{1,0:T(8,128)(2,1)} %get-tuple-element.34, ...), kind=kOutput, calls=%fused_computation.21 | convolution fusion | flops 34502344704 | bytes 41943040 | tf_op jit(solution)/shard_map/dot_general | solution.py:34
  923.4 39.0 %reduce-scatter.6.cloned.1.call-done = bf16[256,4608]{1,0:T(8,128)(2,1)} async-done(((bf16[2048,4608]{1,0:T(8,128)(2,1)}), bf16[256,4608]{1,0:T(8,128)(2,1)}) %reduce-scatter.6.cloned.1.call-update) | async-done | bytes 2359312 | tf_op jit(solution)/shard_map/reduce_scatter | solution.py:514
  967.7 18.6 %fusion.67 = (f32[2048]{0:T(1024)S(1)}, f32[512]{0:T(512)S(1)}, f32[512,2048]{1,0:T(8,128)}) fusion(bf16[512,2048]{1,0:T(8,128)(2,1)S(1)} %copy-done.3, f32[512]{0:T(512)S(1)} %copy-done.22, f32[2048]{0:T(1024)S(1)} %bitcast.60, f32[512,2048]{1,0:T(8,128)} %fusion.54, bf16[512,4608]{1,0:T(8,128)(2,1)} %attend_back.2, ...), kind=kOutput, calls=%fused_computation.70 | convolution fusion | flops 9672062976 | bytes 34099200 | tf_op jit(solution)/shard_map/dot_general | solution.py:40
  1005.7 16.1 %collective-permute-done.21 = f32[2,2048]{1,0:T(2,128)S(1)} collective-permute-done((f32[2,2048]{1,0:T(2,128)S(1)}, f32[2,2048]{1,0:T(2,128)S(1)}, u32[]{:S(2)}, u32[]{:S(2)}) %collective-permute-start.21) | collective-permute-done | bytes 16416 | tf_op jit(solution)/shard_map/ppermute | solution.py:444
  1040.6 117.0 %reduce-scatter.12.cloned.1.call-done = bf16[256,4096]{1,0:T(8,128)(2,1)} async-done(((bf16[2048,4096]{1,0:T(8,128)(2,1)}), bf16[256,4096]{1,0:T(8,128)(2,1)}) %reduce-scatter.12.cloned.1.call-update) | async-done | bytes 2097168 | tf_op jit(solution)/shard_map/reduce_scatter | solution.py:514
  1161.7 61.1 %reduce-scatter.10.cloned.1.call-done = bf16[256,1536]{1,0:T(8,128)(2,1)} async-done(((bf16[2048,1536]{1,0:T(8,128)(2,1)}), bf16[256,1536]{1,0:T(8,128)(2,1)}) %reduce-scatter.10.cloned.1.call-update) | async-done | bytes 786448 | tf_op jit(solution)/shard_map/reduce_scatter | solution.py:514
  (218 shorter events, 392.9 us)
Async XLA Ops:
  7.2 184.3 %all-gather.7.cloned.1.call-start = ((), (), s32[]{:S(2)}) async-start(), calls=%async_computation.5 | async-start | bytes 9437184 | tf_op jit(solution)/shard_map/all_gather | solution.py:460
  12.2 205.0 %all-gather.9.cloned.1.call-start = ((), (), s32[]{:S(2)}) async-start(), calls=%async_computation.6 | async-start | bytes 28311552 | tf_op jit(solution)/shard_map/all_gather | solution.py:465
  12.2 28.5 %collective-permute-start = (bf16[256,2048]{1,0:T(8,128)(2,1)}, bf16[256,2048]{1,0:T(8,128)(2,1)S(1)}, u32[]{:S(2)}, u32[]{:S(2)}) collective-permute-start(bf16[256,2048]{1,0:T(8,128)(2,1)} %copy-done.9), channel_id=1, source_target_pairs={{0,1},{1,2},{2,3},{3,0},{4,5},{5,6},{6,7},{7,4},{8,9},{9,10},{10,1... | collective-permute-start | bytes 3145736 | tf_op jit(solution)/shard_map/ppermute | solution.py:423
  94.1 215.3 %all-gather.11.cloned.1.call-start = ((), (), s32[]{:S(2)}) async-start(), calls=%async_computation.7 | async-start | bytes 18874368 | tf_op jit(solution)/shard_map/all_gather | solution.py:467
  97.3 268.1 %all-gather.13.cloned.1.call-start = ((), (), s32[]{:S(2)}) async-start(), calls=%async_computation.8 | async-start | bytes 9437184 | tf_op jit(solution)/shard_map/all_gather | solution.py:468
  97.9 823.4 %reduce-scatter.8.cloned.1.call-start = ((), (), s32[]{:S(2)}) async-start(), calls=%async_computation.10 | async-start | bytes 9437184 | tf_op jit(solution)/shard_map/reduce_scatter | solution.py:514
  98.0 47.1 %collective-permute-start.9 = (bf16[512,2048]{1,0:T(8,128)(2,1)}, bf16[512,2048]{1,0:T(8,128)(2,1)S(1)}, u32[]{:S(2)}, u32[]{:S(2)}) collective-permute-start(bf16[512,2048]{1,0:T(8,128)(2,1)} %param.21), channel_id=1, source_target_pairs={{0,1},{1,2},{2,3},{3,0},{4,5},{5,6},{6,7},{7,4},{8,9},{9,10},{10,1... | collective-permute-start | bytes 6291464 | tf_op jit(solution)/shard_map/ppermute | solution.py:423
  145.1 46.1 %collective-permute-start.11 = (bf16[512,2048]{1,0:T(8,128)(2,1)S(1)}, bf16[512,2048]{1,0:T(8,128)(2,1)}, u32[]{:S(2)}, u32[]{:S(2)}) collective-permute-start(bf16[512,2048]{1,0:T(8,128)(2,1)S(1)} %collective-permute-done.9), channel_id=1, source_target_pairs={{0,1},{1,2},{2,3},{3,0},{4,5},{5,6},{6,7},{7,4},{8,9},{9,10},{10,1... | collective-permute-start | bytes 6291464 | tf_op jit(solution)/shard_map/ppermute | solution.py:423
  191.3 387.4 %collective-permute-start.13 = (bf16[512,2048]{1,0:T(8,128)(2,1)}, bf16[512,2048]{1,0:T(8,128)(2,1)}, u32[]{:S(2)}, u32[]{:S(2)}) collective-permute-start(bf16[512,2048]{1,0:T(8,128)(2,1)} %collective-permute-done.11), channel_id=1, source_target_pairs={{0,1},{1,2},{2,3},{3,0},{4,5},{5,6},{6,7},{7,4},{8,9},{9,10},{10,1... | collective-permute-start | bytes 6291464 | tf_op jit(solution)/shard_map/ppermute | solution.py:423
  272.3 108.2 %collective-permute-start.3 = (bf16[512,2048]{1,0:T(8,128)(2,1)S(1)}, bf16[512,2048]{1,0:T(8,128)(2,1)}, u32[]{:S(2)}, u32[]{:S(2)}) collective-permute-start(bf16[512,2048]{1,0:T(8,128)(2,1)S(1)} %multiply_convert_fusion.12), channel_id=1, source_target_pairs={{0,1},{1,2},{2,3},{3,0},{4,5},{5,6},{6,7},{7,4},{8,9},{9,10},{10,1... | collective-permute-start | bytes 6291464 | tf_op jit(solution)/shard_map/ppermute | solution.py:423
  380.5 52.8 %collective-permute-start.5 = (bf16[512,2048]{1,0:T(8,128)(2,1)}, bf16[512,2048]{1,0:T(8,128)(2,1)S(1)}, u32[]{:S(2)}, u32[]{:S(2)}) collective-permute-start(bf16[512,2048]{1,0:T(8,128)(2,1)} %collective-permute-done.3), channel_id=1, source_target_pairs={{0,1},{1,2},{2,3},{3,0},{4,5},{5,6},{6,7},{7,4},{8,9},{9,10},{10,1... | collective-permute-start | bytes 6291464 | tf_op jit(solution)/shard_map/ppermute | solution.py:423
  421.8 54.7 %collective-permute-start.10 = (bf16[512,2048]{1,0:T(8,128)(2,1)}, bf16[512,2048]{1,0:T(8,128)(2,1)}, u32[]{:S(2)}, u32[]{:S(2)}) collective-permute-start(bf16[512,2048]{1,0:T(8,128)(2,1)} %fusion.93), channel_id=1, source_target_pairs={{0,1},{1,2},{2,3},{3,0},{4,5},{5,6},{6,7},{7,4},{8,9},{9,10},{10,1... | collective-permute-start | bytes 6291464 | tf_op jit(solution)/shard_map/ppermute | solution.py:423
  431.6 89.7 %collective-permute-start.4 = (bf16[512,2048]{1,0:T(8,128)(2,1)S(1)}, bf16[512,2048]{1,0:T(8,128)(2,1)S(1)}, u32[]{:S(2)}, u32[]{:S(2)}) collective-permute-start(bf16[512,2048]{1,0:T(8,128)(2,1)S(1)} %convolution_convert_fusion.3), channel_id=1, source_target_pairs={{0,1},{1,2},{2,3},{3,0},{4,5},{5,6},{6,7},{7,4},{8,9},{9,10},{10,1... | collective-permute-start | bytes 6291464 | tf_op jit(solution)/shard_map/ppermute | solution.py:423
  433.3 133.1 %collective-permute-start.7 = (bf16[512,2048]{1,0:T(8,128)(2,1)S(1)}, bf16[512,2048]{1,0:T(8,128)(2,1)}, u32[]{:S(2)}, u32[]{:S(2)}) collective-permute-start(bf16[512,2048]{1,0:T(8,128)(2,1)S(1)} %collective-permute-done.5), channel_id=1, source_target_pairs={{0,1},{1,2},{2,3},{3,0},{4,5},{5,6},{6,7},{7,4},{8,9},{9,10},{10,1... | collective-permute-start | bytes 6291464 | tf_op jit(solution)/shard_map/ppermute | solution.py:423
  491.4 119.9 %collective-permute-start.12 = (bf16[512,2048]{1,0:T(8,128)(2,1)}, bf16[512,2048]{1,0:T(8,128)(2,1)}, u32[]{:S(2)}, u32[]{:S(2)}) collective-permute-start(bf16[512,2048]{1,0:T(8,128)(2,1)} %add_convert_fusion.1), channel_id=1, source_target_pairs={{0,1},{1,2},{2,3},{3,0},{4,5},{5,6},{6,7},{7,4},{8,9},{9,10},{10,1... | collective-permute-start | bytes 6291464 | tf_op jit(solution)/shard_map/ppermute | solution.py:423
  531.4 124.8 %collective-permute-start.6 = (bf16[512,2048]{1,0:T(8,128)(2,1)}, bf16[512,2048]{1,0:T(8,128)(2,1)S(1)}, u32[]{:S(2)}, u32[]{:S(2)}) collective-permute-start(bf16[512,2048]{1,0:T(8,128)(2,1)} %add_convert_fusion.4), channel_id=1, source_target_pairs={{0,1},{1,2},{2,3},{3,0},{4,5},{5,6},{6,7},{7,4},{8,9},{9,10},{10,1... | collective-permute-start | bytes 6291464 | tf_op jit(solution)/shard_map/ppermute | solution.py:423
  613.9 87.2 %collective-permute-start.14 = (bf16[512,2048]{1,0:T(8,128)(2,1)S(1)}, bf16[512,2048]{1,0:T(8,128)(2,1)S(1)}, u32[]{:S(2)}, u32[]{:S(2)}) collective-permute-start(bf16[512,2048]{1,0:T(8,128)(2,1)S(1)} %add_convert_fusion), channel_id=1, source_target_pairs={{0,1},{1,2},{2,3},{3,0},{4,5},{5,6},{6,7},{7,4},{8,9},{9,10},{10,1... | collective-permute-start | bytes 6291464 | tf_op jit(solution)/shard_map/ppermute | solution.py:423
  658.2 87.2 %collective-permute-start.8 = (bf16[512,2048]{1,0:T(8,128)(2,1)}, bf16[512,2048]{1,0:T(8,128)(2,1)}, u32[]{:S(2)}, u32[]{:S(2)}) collective-permute-start(bf16[512,2048]{1,0:T(8,128)(2,1)} %add_convert_fusion.3), channel_id=1, source_target_pairs={{0,1},{1,2},{2,3},{3,0},{4,5},{5,6},{6,7},{7,4},{8,9},{9,10},{10,1... | collective-permute-start | bytes 6291464 | tf_op jit(solution)/shard_map/ppermute | solution.py:423
  762.6 199.8 %reduce-scatter.6.cloned.1.call-start = ((), (), s32[]{:S(2)}) async-start(), calls=%async_computation.9 | async-start | bytes 21233664 | tf_op jit(solution)/shard_map/reduce_scatter | solution.py:514
  814.7 223.1 %reduce-scatter.14.cloned.1.call-start = ((), (), s32[]{:S(2)}) async-start(), calls=%async_computation.13 | async-start | bytes 9437184 | tf_op jit(solution)/shard_map/reduce_scatter | solution.py:514
  838.5 319.1 %reduce-scatter.12.cloned.1.call-start = ((), (), s32[]{:S(2)}) async-start(), calls=%async_computation.12 | async-start | bytes 18874368 | tf_op jit(solution)/shard_map/reduce_scatter | solution.py:514
  890.2 332.6 %reduce-scatter.10.cloned.1.call-start = ((), (), s32[]{:S(2)}) async-start(), calls=%async_computation.11 | async-start | bytes 7077888 | tf_op jit(solution)/shard_map/reduce_scatter | solution.py:514
  995.5 27.1 %collective-permute-start.16 = (bf16[256,2048]{1,0:T(8,128)(2,1)}, bf16[256,2048]{1,0:T(8,128)(2,1)S(1)}, u32[]{:S(2)}, u32[]{:S(2)}) collective-permute-start(bf16[256,2048]{1,0:T(8,128)(2,1)} %add_convert_fusion.6), channel_id=1, source_target_pairs={{0,1},{1,2},{2,3},{3,0},{4,5},{5,6},{6,7},{7,4},{8,9},{9,10},{10,1... | collective-permute-start | bytes 3145736 | tf_op jit(solution)/shard_map/ppermute | solution.py:423
  1025.3 197.5 %collective-permute-start.17 = (bf16[256,2048]{1,0:T(8,128)(2,1)}, bf16[256,2048]{1,0:T(8,128)(2,1)S(1)}, u32[]{:S(2)}, u32[]{:S(2)}) collective-permute-start(bf16[256,2048]{1,0:T(8,128)(2,1)} %add_convert_fusion.5), channel_id=1, source_target_pairs={{0,1},{1,2},{2,3},{3,0},{4,5},{5,6},{6,7},{7,4},{8,9},{9,10},{10,1... | collective-permute-start | bytes 3145736 | tf_op jit(solution)/shard_map/ppermute | solution.py:423
  (48 other events, 1441.3 us)
Sparse Core Ops, SparseCore 0:
  12.3 56.9 all-gather.6
  94.1 122.9 all-gather.8
  219.6 89.7 all-gather.10
  311.1 54.2 all-gather.12
  762.8 69.6 reduce-scatter.7
  836.0 126.4 reduce-scatter.5
  965.9 71.8 reduce-scatter.13
  1041.4 116.1 reduce-scatter.11
  1161.0 61.7 reduce-scatter.9

commit v2 on v1

--- a/solution.py
+++ b/solution.py
@@ -419,8 +419,116 @@
     )(query, key, value, grad, cosine, sine)
 
 
+TILE = 256
+
+
+def unit_kernel(norm_ref, grad_ref, gate_ref, up_ref, down_ref, activ_ref, pre_ref):
+    rows = norm_ref[...]
+    gate = jnp.dot(rows, gate_ref[...], preferred_element_type=jnp.float32)
+    up = jnp.dot(rows, up_ref[...], preferred_element_type=jnp.float32)
+    grad_activ = jnp.dot(grad_ref[...], down_ref[...], preferred_element_type=jnp.float32)
+    sigma = jax.nn.sigmoid(gate)
+    swish = gate * sigma
+    activ_ref[...] = (swish * up).astype(jnp.bfloat16)
+    grad_gate = grad_activ * up * sigma * (1.0 + gate * (1.0 - sigma))
+    place = pl.multiple_of(pl.program_id(0) * TILE, TILE)
+    units = pre_ref.shape[1] // 2
+    pre_ref[:, pl.ds(place, TILE)] = grad_gate.astype(jnp.bfloat16)
+    pre_ref[:, pl.ds(units + place, TILE)] = (grad_activ * swish).astype(jnp.bfloat16)
+
+
+def hidden_units_pass(normed, grads, gate_up, down):
+    rows, width = normed.shape
+    units = down.shape[1]
+    steps = units // TILE
+    whole = pl.BlockSpec((rows, width), lambda step: (0, 0))
+
+    def tile(offset):
+        return pl.BlockSpec((width, TILE), lambda step: (0, offset + step))
+
+    return pl.pallas_call(
+        unit_kernel,
+        grid=(steps,),
+        in_specs=[whole, whole, tile(0), tile(steps), tile(0)],
+        out_specs=[
+            pl.BlockSpec((rows, TILE), lambda step: (0, step)),
+            pl.BlockSpec((rows, 2 * units), lambda step: (0, 0)),
+        ],
+        out_shape=[
+            jax.ShapeDtypeStruct((rows, units), jnp.bfloat16),
+            jax.ShapeDtypeStruct((rows, 2 * units), jnp.bfloat16),
+        ],
+        name="units",
+        cost_estimate=pl.CostEstimate(
+            flops=rows * width * units, transcendentals=0, bytes_accessed=4 * rows * width
+        ),
+    )(normed, grads, gate_up, gate_up, down)
+
+
+def rows_kernel(left_ref, right_ref, out_ref):
+    out_ref[...] = dot_last(left_ref[...], right_ref[...]).astype(out_ref.dtype)
+
+
+def times_rows(left, right, dtype):
+    rows, depth = left.shape
+    width = right.shape[0]
+    return pl.pallas_call(
+        rows_kernel,
+        grid=(width // TILE,),
+        in_specs=[
+            pl.BlockSpec((rows, depth), lambda step: (0, 0)),
+            pl.BlockSpec((TILE, depth), lambda step: (step, 0)),
+        ],
+        out_specs=pl.BlockSpec((rows, TILE), lambda step: (0, step)),
+        out_shape=jax.ShapeDtypeStruct((rows, width), dtype),
+        name="sums",
+        cost_estimate=pl.CostEstimate(
+            flops=rows * width * depth // 4, transcendentals=0, bytes_accessed=rows * width
+        ),
+    )(left, right)
+
+
 def shift(values, count):
     return lax.ppermute(values, "tensor", [(i, (i + 1) % count) for i in range(count)])
+
+
+def after(values, *earlier):
+    return lax.optimization_barrier((values,) + earlier)[0]
+
+
+PEERS = 8
+ORDER = (0, 2, 4, 6, 1, 3, 5, 7)
+
+
+def peer(values, hop):
+    return lax.ppermute(values, "dp", [(i, i ^ hop) for i in range(PEERS)])
+
+
+def by_peer(values):
+    width = values.shape[1] // PEERS
+    blocks = [values[:, k * width : (k + 1) * width] for k in range(PEERS)]
+    me = lax.axis_index("dp")
+    for hop in (1, 2, 4):
+        blocks = [jnp.where(me & hop, blocks[k ^ hop], blocks[k]) for k in range(PEERS)]
+    half = PEERS // 2
+    near = jnp.concatenate([blocks[k] for k in ORDER[:half]], axis=1)
+    far = jnp.concatenate([blocks[k] for k in ORDER[half:]], axis=1)
+    return near, far
+
+
+def corner_step(kept):
+    rows = kept.shape[0] // 4
+    half = rows // 2
+    mine, over_x, over_y, corner = [kept[k * rows : (k + 1) * rows] for k in range(4)]
+    from_y, from_x = peer(corner[:half], 4), peer(corner[half:], 2)
+    over_x = jnp.concatenate([over_x[:half] + from_y, over_x[half:]], axis=0)
+    over_y = jnp.concatenate([over_y[:half], over_y[half:] + from_x], axis=0)
+    return mine, over_x, over_y
+
+
+def cross_step(mine, over_x, over_y):
+    over_x, over_y = peer(over_x, 2), peer(over_y, 4)
+    return mine.astype(jnp.float32) + over_x.astype(jnp.float32) + over_y.astype(jnp.float32)
 
 
 def travel(values, count):
@@ -464,50 +572,56 @@
     )
     rest = lax.all_gather(rest_shard, "dp", axis=0, tiled=True)
     wide = (count - 1) * heads
-    gate_up = lax.all_gather(jnp.concatenate([w_gate, w_up], axis=1), "dp", axis=0, tiled=True)
-    down = lax.all_gather(w_down, "dp", axis=0, tiled=True)
-    cotangents = travel(cotangent, count)
+    gate_up_shard = after(jnp.concatenate([w_gate, w_up], axis=1), rest_shard)
+    gate_up = lax.all_gather(gate_up_shard, "dp", axis=0, tiled=True)
+    down = lax.all_gather(after(w_down, rest_shard), "dp", axis=0, tiled=True)
 
     source = tokens.astype(jnp.float32)
     inverse_one = lax.rsqrt(jnp.mean(source * source, axis=-1, keepdims=True) + eps)
     normed_one = (source * inverse_one * attn_scale).astype(jnp.bfloat16)
+    near_one, far_one = by_peer(normed_one)
     cosine, sine = lane_tables()
     own_qkv = jnp.dot(normed_one, own[:, : 3 * heads], preferred_element_type=jnp.float32)
     own_query, own_key, own_value, own_mixed = attention(own_qkv, cosine, sine)
+    cotangents = [cotangent, shift(after(cotangent, others[-1]), count)]
+    for _ in range(count - 2):
+        cotangents.append(shift(after(cotangents[-1], own_mixed), count))
+    rest = after(rest, *cotangents[:-1])
     rest_qkv = jnp.dot(normed_one, rest[:, : 3 * wide], preferred_element_type=jnp.float32)
     rest_query, rest_key, rest_value, rest_mixed = attention(rest_qkv, cosine, sine)
     branch = contract_cols(own_mixed, own[:, 3 * heads :])
     branch = branch + contract_cols(rest_mixed, rest[:, 3 * wide :])
-    hidden = source + branch
+    hidden = source + after(branch, cotangents[-1])
     inverse_two = lax.rsqrt(jnp.mean(hidden * hidden, axis=-1, keepdims=True) + eps)
     normed_two = (hidden * inverse_two * mlp_scale).astype(jnp.bfloat16)
 
     normed = travel(normed_two, count)
-    activs, pres, mlp_parts, norm_parts = [], [], [], []
-    for normed_rows, grad_rows in zip(normed, cotangents):
-        both = jnp.dot(normed_rows, gate_up, preferred_element_type=jnp.float32)
-        gate, up = both[:, :hidden_units], both[:, hidden_units:]
-        sigma = jax.nn.sigmoid(gate)
-        swish = gate * sigma
-        activ = (swish * up).astype(jnp.bfloat16)
-        grad_activ = jnp.dot(grad_rows, down, preferred_element_type=jnp.float32)
-        grad_gate_pre = (grad_activ * up * sigma * (1.0 + gate * (1.0 - sigma))).astype(
-            jnp.bfloat16
-        )
-        grad_up_pre = (grad_activ * swish).astype(jnp.bfloat16)
-        pre = jnp.concatenate([grad_gate_pre, grad_up_pre], axis=1)
+    activs, pres, norm_parts = [], [], []
+    arrived = None
+    for j in range(count):
+        earlier = (normed[2],) if j == 1 else (norm_total,) if j == 3 else ()
+        rows = after(normed[j], *earlier)
+        activ, pre = hidden_units_pass(rows, cotangents[j], gate_up, down)
+        norm_part = times_rows(pre, gate_up, jnp.float32)
+        if j == 1:
+            norm_total = norm_part.astype(jnp.bfloat16)
+        elif j > 1:
+            arrived = shift(norm_total, count)
+            norm_total = (arrived.astype(jnp.float32) + norm_part).astype(jnp.bfloat16)
         activs.append(activ)
         pres.append(pre)
-        norm_parts.append(contract_cols(pre, gate_up))
-        mlp_parts.append(contract_cols(activ, down))
-    grad_normed_two = ring_sum(norm_parts, count)
-    mlp_branch = ring_sum(mlp_parts, count)
-    block_out = (hidden + mlp_branch).astype(jnp.bfloat16)
+        norm_parts.append(norm_part)
+    arrived = shift(norm_total, count)
     all_normed = jnp.concatenate(normed, axis=0)
     all_cotangents = jnp.concatenate(cotangents, axis=0)
-    grad_gate_up_w = contract_rows(all_normed, jnp.concatenate(pres, axis=0)).astype(jnp.bfloat16)
+    activs[-1] = after(activs[-1], norm_total)
     grad_down_w = contract_rows(all_cotangents, jnp.concatenate(activs, axis=0)).astype(
         jnp.bfloat16
+    )
+    pres[-1] = after(pres[-1], grad_down_w, norm_total)
+    grad_gate_up_w = contract_rows(all_normed, jnp.concatenate(pres, axis=0)).astype(jnp.bfloat16)
+    grad_normed_two = arrived.astype(jnp.float32) + after(
+        norm_parts[0], grad_gate_up_w, grad_down_w
     )
 
     def over_dp(values):
@@ -520,33 +634,63 @@
     grad_hidden = cotangent.astype(jnp.float32) + grad_hidden_norm
     grad_branch = grad_hidden.astype(jnp.bfloat16)
     all_mixed = jnp.concatenate([own_mixed, rest_mixed], axis=1)
-    grad_output_w = contract_rows(grad_branch, all_mixed).astype(jnp.bfloat16)
+    near_branch, far_branch = by_peer(grad_branch)
+    output_far = contract_rows(far_branch, all_mixed).astype(jnp.bfloat16)
     rest_grad = jnp.dot(
-        grad_branch, rest[:, 3 * wide :], preferred_element_type=jnp.float32
+        after(grad_branch, output_far), rest[:, 3 * wide :], preferred_element_type=jnp.float32
     ).astype(jnp.bfloat16)
+    output_near = contract_rows(near_branch, after(all_mixed, rest_grad))
+    output_near = (output_near + peer(output_far, 1).astype(jnp.float32)).astype(jnp.bfloat16)
+    output_parts = corner_step(output_near)
+    rest_grad = after(rest_grad, output_near, grad_down)
+    rest_pre = attention_back(rest_query, rest_key, rest_value, rest_grad, cosine, sine)
+
+    def mlp_part(j, stage):
+        return times_rows(after(activs[j], stage), down, jnp.bfloat16)
+
+    mlp_arrived = shift(mlp_part(1, grad_branch), count)
+    mlp_next = mlp_part(2, output_far)
+    rest_pre = after(rest_pre, mlp_arrived, *output_parts)
+    mlp_total = (mlp_arrived.astype(jnp.float32) + after(mlp_next, rest_pre)).astype(jnp.bfloat16)
+    mlp_arrived = shift(mlp_total, count)
+    rest_far = contract_rows(far_one, rest_pre).astype(jnp.bfloat16)
+    output_sum = cross_step(*output_parts)
+    rest_later = after(rest_pre, rest_far)
+    grad_normed_one = contract_cols(rest_later, rest[:, : 3 * wide])
+    rest_later = after(rest_later, grad_normed_one, output_sum)
+    rest_near = contract_rows(near_one, rest_later) + peer(rest_far, 1).astype(jnp.float32)
+    rest_near = rest_near.astype(jnp.bfloat16)
+    rest_parts = corner_step(rest_near)
     own_grad = jnp.dot(
-        grad_branch, own[:, 3 * heads :], preferred_element_type=jnp.float32
+        after(grad_branch, rest_near), own[:, 3 * heads :], preferred_element_type=jnp.float32
     ).astype(jnp.bfloat16)
-    rest_pre = attention_back(rest_query, rest_key, rest_value, rest_grad, cosine, sine)
-    rest_grad_w = contract_rows(normed_one, rest_pre).astype(jnp.bfloat16)
     own_pre = attention_back(own_query, own_key, own_value, own_grad, cosine, sine)
-    own_grad_w = contract_rows(normed_one, own_pre).astype(jnp.bfloat16)
-    grad_normed_one = contract_cols(rest_pre, rest[:, : 3 * wide])
-    grad_normed_one = grad_normed_one + contract_cols(own_pre, own[:, : 3 * heads])
+    own_pre = after(own_pre, mlp_arrived, grad_gate_up, *rest_parts)
+    mlp_next = after(mlp_part(3, rest_far), own_pre)
+    mlp_total = (mlp_arrived.astype(jnp.float32) + mlp_next).astype(jnp.bfloat16)
+    mlp_total = shift(mlp_total, count).astype(jnp.float32) + mlp_part(0, rest_near)
+    rest_sum = cross_step(*rest_parts)
+    own_far = contract_rows(far_one, own_pre).astype(jnp.bfloat16)
+    own_later = after(own_pre, own_far)
+    grad_normed_one = grad_normed_one + contract_cols(own_later, own[:, : 3 * heads])
+    own_near = contract_rows(near_one, own_later) + peer(own_far, 1).astype(jnp.float32)
+    own_sum = cross_step(*corner_step(own_near.astype(jnp.bfloat16)))
+    block_out = (hidden + mlp_total).astype(jnp.bfloat16)
+
     grad_source_norm, attn_gain_part = norm_back(grad_normed_one, source, inverse_one, attn_scale)
     grad_tokens = (grad_hidden + grad_source_norm).astype(jnp.bfloat16)
 
-    output_sum = over_dp(grad_output_w)
-    rest_sum = over_dp(rest_grad_w)
-    own_sum = over_dp(own_grad_w)
-    slots = [jnp.concatenate([own_sum, output_sum[:, :heads]], axis=1)]
-    for j in range(1, count):
+    def group_slot(j):
+        if not j:
+            return own_sum
         columns = [rest_sum[:, k * wide + (j - 1) * heads : k * wide + j * heads] for k in range(3)]
-        slots.append(jnp.concatenate(columns + [output_sum[:, j * heads : (j + 1) * heads]], axis=1))
-    grads = ring_sum([slot.astype(jnp.float32) for slot in slots], count)
-    grad_query, grad_key, grad_value, grad_output = [
-        grads[:, k * heads : (k + 1) * heads] for k in range(4)
-    ]
+        return jnp.concatenate(columns, axis=1)
+
+    qkv = ring_sum([group_slot(j) for j in range(count)], count)
+    grad_query, grad_key, grad_value = [qkv[:, k * heads : (k + 1) * heads] for k in range(3)]
+    grad_output = ring_sum(
+        [output_sum[:, j * heads : (j + 1) * heads].astype(jnp.float32) for j in range(count)], count
+    )
     gain_parts = sum_all(
         jnp.stack([attn_gain_part, mlp_gain_part]), (("dp", dp_count), ("tensor", count))
     )
@@ -568,14 +712,10 @@
     )
 
 
-def power_of_two(number):
-    return number & (number - 1) == 0
-
-
 def local(tokens, w_query, *others):
     axes = (lax.axis_size("dp"), lax.axis_size("tensor"))
     whole = tokens.shape[0] == LEN and w_query.shape[1] % PAIR == 0
-    if whole and axes[1] > 1 and all(power_of_two(size) for size in axes):
+    if whole and axes[0] == PEERS and axes[1] == 4:
         return token_parallel(tokens, w_query, *others)
     return tensor_parallel(tokens, w_query, *others)
 

time: 1240 us -> 1060 us (0.85)
  waiting for transfers between devices: 681 us -> 454 us
  matrix products: 371 us -> 176 us
  Pallas kernels: 73.1 us -> 264 us
  other arithmetic: 41.9 us -> 79.8 us
    reduce_scatter x5 -> x2, waiting for transfers between devices: 223 us -> 0.01 us  [over_dp(): return lax.psum_scatter(values, 'dp', scatter_dimension=0, tiled=True)]
    pallas_call x0 -> x12, Pallas kernels: none -> 191 us  [the longest x8 108 us: times_rows(): pl.pallas_call(rows_kernel, grid=(width // TILE,), in_specs=[pl.BlockSpec...]
    dot_general x12 -> x4, matrix products: 136 us -> 36.2 us  [contract_cols(): lax.dot_general(left, right, (((1,), (1,)), ((), ())), preferred_element_...]
    dot_general x10 -> x2, matrix products: 112 us -> 12.1 us  [the longest x1 8.47 us: token_parallel(): jnp.dot(after(grad_branch, output_far), rest[:, 3 * wide:], preferred_ele...]
    all_gather x2, waiting for transfers between devices: 77 us -> 0.01 us  [the longest x1 0.01 us: token_parallel(): gate_up = lax.all_gather(gate_up_shard, 'dp', axis=0, tiled=True)]
    ppermute x0 -> x15, waiting for transfers between devices: none -> 61.6 us  [peer(): return lax.ppermute(values, 'dp', [(i, i ^ hop) for i in range(PEERS)])]
    convert_element_type x0 -> x9, other arithmetic: none -> 29.5 us  [the longest x2 9.84 us: token_parallel(): norm_total = (arrived.astype(jnp.float32) + norm_part).astype(jnp.bfloat16)]
    ppermute x5, waiting for transfers between devices: 21.6 us -> 50.3 us  [sum_all(): lax.ppermute(values, name, [(i, i ^ hop) for i in range(count)])]
  transfers between devices with their start and end apart: 32 -> 47, of which waited for: 23 -> 23; matrix products, arithmetic and copies ran while one was open for 33% -> 22% of each run, Pallas kernels for 6% -> 22%
where the time goes in v2:
time: 1060 us; the launch traced here: 1050 us
  waiting for transfers between devices  454 us (43%)
  Pallas kernels  264 us (25%)
  matrix products  176 us (17%)
  other arithmetic  79.8 us (8%)
  local copies, waits for them, and re-layouts  29.4 us (3%)
  starting transfers between devices  26 us (2%)
  between operations  15.2 us (1%)
    ppermute x21, waiting for transfers between devices, shift(): lax.ppermute(values, 'tensor', [(i, (i + 1) % count) for i in range(count)])  331 us
    pallas_call x8, Pallas kernels, times_rows(): pl.pallas_call(rows_kernel, grid=(width // TILE,), in_specs=[pl.BlockSpec...  108 us
    dot_general x8, matrix products, contract_rows(): lax.dot_general(left, right, (((0,), (0,)), ((), ())), preferred_element_...  103 us
    pallas_call x4, Pallas kernels, hidden_units_pass(): pl.pallas_call(unit_kernel, grid=(steps,), in_specs=[whole, whole, tile(0...  83.6 us
    ppermute x15, waiting for transfers between devices, peer(): return lax.ppermute(values, 'dp', [(i, i ^ hop) for i in range(PEERS)])  61.6 us
    ppermute x5, waiting for transfers between devices, sum_all(): lax.ppermute(values, name, [(i, i ^ hop) for i in range(count)])  50.3 us
    pallas_call x2, Pallas kernels, attention_back(): pl.pallas_call(backward_kernel, grid=(columns // PAIR,), in_specs=[pair_b...  37 us
    dot_general x4, matrix products, contract_cols(): lax.dot_general(left, right, (((1,), (1,)), ((), ())), preferred_element_...  36.2 us
  transfers between devices with their start and end apart: 47, of which 23 were waited for; matrix products, arithmetic and copies ran while one was open for 22% of the time, Pallas kernels for 22%

profile of v2, /device:TPU:0, one launch (start us, length us, event | category | flops | bytes accessed | tf_op | source)
XLA Modules:
  0.0 1052.5 jit_solution(13500887951498345470)
XLA Ops:
  15.3 25.4 %collective-permute-done = bf16[256,2048]{1,0:T(8,128)(2,1)S(1)} collective-permute-done((bf16[256,2048]{1,0:T(8,128)(2,1)}, bf16[256,2048]{1,0:T(8,128)(2,1)S(1)}, u32[]{:S(2)}, u32[]{:S(2)}) %collective-permute-start) | collective-permute-done | bytes 1048608 | tf_op jit(solution)/shard_map/ppermute | solution.py:492
  40.7 26.1 %collective-permute-done.1 = bf16[256,2048]{1,0:T(8,128)(2,1)S(1)} collective-permute-done((bf16[256,2048]{1,0:T(8,128)(2,1)S(1)}, bf16[256,2048]{1,0:T(8,128)(2,1)S(1)}, u32[]{:S(2)}, u32[]{:S(2)}) %collective-permute-start.1) | collective-permute-done | bytes 1048608 | tf_op jit(solution)/shard_map/ppermute | solution.py:492
  66.9 25.2 %collective-permute-done.2 = bf16[256,2048]{1,0:T(8,128)(2,1)S(1)} collective-permute-done((bf16[256,2048]{1,0:T(8,128)(2,1)S(1)}, bf16[256,2048]{1,0:T(8,128)(2,1)S(1)}, u32[]{:S(2)}, u32[]{:S(2)}) %collective-permute-start.2) | collective-permute-done | bytes 1048608 | tf_op jit(solution)/shard_map/ppermute | solution.py:492
  130.1 27.8 %collective-permute-done.3.grad_ref = bf16[512,2048]{1,0:T(8,128)(2,1)} collective-permute-done((bf16[512,2048]{1,0:T(8,128)(2,1)}, bf16[512,2048]{1,0:T(8,128)(2,1)}, u32[]{:S(2)}, u32[]{:S(2)}) %collective-permute-start.3) | collective-permute-done | bytes 2097184 | tf_op jit(solution)/shard_map/ppermute | solution.py:492
  162.9 44.1 %collective-permute-done.4.grad_ref = bf16[512,2048]{1,0:T(8,128)(2,1)} collective-permute-done((bf16[512,2048]{1,0:T(8,128)(2,1)}, bf16[512,2048]{1,0:T(8,128)(2,1)}, u32[]{:S(2)}, u32[]{:S(2)}) %collective-permute-start.4) | collective-permute-done | bytes 2097184 | tf_op jit(solution)/shard_map/ppermute | solution.py:492
  217.2 16.5 %fusion.10.q_ref.k_ref.v_ref = f32[512,4608]{1,0:T(8,128)} fusion(bf16[512,2048]{1,0:T(8,128)(2,1)} %fusion.52, bf16[2048,6144]{1,0:T(8,128)(2,1)} %all-gather.9.cloned.1.call-done), kind=kOutput, calls=%fused_computation.11 | convolution fusion | flops 9663676416 | bytes 30408704 | tf_op jit(solution)/shard_map/dot_general | solution.py:590
  233.7 25.8 %attend.3 = (bf16[512,1536]{1,0:T(8,128)(2,1)}, bf16[512,1536]{1,0:T(8,128)(2,1)}, bf16[512,1536]{1,0:T(8,128)(2,1)}, bf16[512,1536]{1,0:T(8,128)(2,1)}) custom-call(f32[512,4608]{1,0:T(8,128)} %fusion.10.q_ref.k_ref.v_ref, f32[512,4608]{1,0:T(8,128)} %fusion.10.q_ref.k_ref.v_ref, f32[512,4608]{1,0:T(8,128)} %fusion.10.q_ref.k_ref.v_ref, ...), custom_call_target="tpu_custom_call" | custom-call | flops 3221225472 | bytes 15728640 | tf_op jit(solution)/shard_map/attend/pallas_call | solution.py:389
  271.6 48.1 %collective-permute-done.6.norm_ref = bf16[512,2048]{1,0:T(8,128)(2,1)S(1)} collective-permute-done((bf16[512,2048]{1,0:T(8,128)(2,1)S(1)}, bf16[512,2048]{1,0:T(8,128)(2,1)S(1)}, u32[]{:S(2)}, u32[]{:S(2)}) %collective-permute-start.6) | collective-permute-done | bytes 2097184 | tf_op jit(solution)/shard_map/ppermute | solution.py:492
  321.1 48.9 %collective-permute-done.7.norm_ref = bf16[512,2048]{1,0:T(8,128)(2,1)} collective-permute-done((bf16[512,2048]{1,0:T(8,128)(2,1)S(1)}, bf16[512,2048]{1,0:T(8,128)(2,1)}, u32[]{:S(2)}, u32[]{:S(2)}) %collective-permute-start.7) | collective-permute-done | bytes 2097184 | tf_op jit(solution)/shard_map/ppermute | solution.py:492
  370.0 20.9 %units.4 = (bf16[512,2048]{1,0:T(8,128)(2,1)}, bf16[512,4096]{1,0:T(8,128)(2,1)}) custom-call(bf16[512,2048]{1,0:T(8,128)(2,1)} %copy-done.18, bf16[512,2048]{1,0:T(8,128)(2,1)} %collective-permute-done.3.grad_ref, bf16[2048,4096]{1,0:T(8,128)(2,1)} %all-gather.11.cloned.1.call-done.gate_ref.up_ref.right_ref, ...), custom_call_target="tpu_custom_call" | custom-call | flops 2147483648 | bytes 4194304 | tf_op jit(solution)/shard_map/units/pallas_call | solution.py:449
  410.8 20.9 %units.5 = (bf16[512,2048]{1,0:T(8,128)(2,1)}, bf16[512,4096]{1,0:T(8,128)(2,1)}) custom-call(bf16[512,2048]{1,0:T(8,128)(2,1)} %collective-permute-done.7.norm_ref, bf16[512,2048]{1,0:T(8,128)(2,1)} %collective-permute-done.4.grad_ref, bf16[2048,4096]{1,0:T(8,128)(2,1)} %all-gather.11.cloned.1.call-done.gate_ref.up_ref.right_ref, ...), custom_call_target="tpu_custom_call" | custom-call | flops 2147483648 | bytes 4194304 | tf_op jit(solution)/shard_map/units/pallas_call | solution.py:449
  466.0 20.9 %units.7 = (bf16[512,2048]{1,0:T(8,128)(2,1)}, bf16[512,4096]{1,0:T(8,128)(2,1)}) custom-call(bf16[512,2048]{1,0:T(8,128)(2,1)} %copy-done.6, bf16[512,2048]{1,0:T(8,128)(2,1)} %grad_ref.1, bf16[2048,4096]{1,0:T(8,128)(2,1)} %all-gather.11.cloned.1.call-done.gate_ref.up_ref.right_ref, ...), custom_call_target="tpu_custom_call" | custom-call | flops 2147483648 | bytes 4194304 | tf_op jit(solution)/shard_map/units/pallas_call | solution.py:449
  486.9 19.0 %collective-permute-done.10.norm_ref = bf16[512,2048]{1,0:T(8,128)(2,1)S(1)} collective-permute-done((bf16[512,2048]{1,0:T(8,128)(2,1)}, bf16[512,2048]{1,0:T(8,128)(2,1)S(1)}, u32[]{:S(2)}, u32[]{:S(2)}) %collective-permute-start.10) | collective-permute-done | bytes 2097184 | tf_op jit(solution)/shard_map/ppermute | solution.py:492
  507.2 20.9 %units.6 = (bf16[512,2048]{1,0:T(8,128)(2,1)}, bf16[512,4096]{1,0:T(8,128)(2,1)}) custom-call(bf16[512,2048]{1,0:T(8,128)(2,1)} %copy-done.19, bf16[512,2048]{1,0:T(8,128)(2,1)} %collective-permute-done.5.grad_ref, bf16[2048,4096]{1,0:T(8,128)(2,1)} %all-gather.11.cloned.1.call-done.gate_ref.up_ref.right_ref, ...), custom_call_target="tpu_custom_call" | custom-call | flops 2147483648 | bytes 4194304 | tf_op jit(solution)/shard_map/units/pallas_call | solution.py:449
  528.1 15.8 %sums.10 = f32[512,2048]{1,0:T(8,128)} custom-call(bf16[512,4096]{1,0:T(8,128)(2,1)} %get-tuple-element.74.left_ref, bf16[2048,4096]{1,0:T(8,128)(2,1)} %all-gather.11.cloned.1.call-done.gate_ref.up_ref.right_ref), custom_call_target="tpu_custom_call" | custom-call | flops 1073741824 | bytes 1048576 | tf_op jit(solution)/shard_map/sums/pallas_call | solution.py:475
  553.5 23.0 %fusion.37 = bf16[2048,2048]{1,0:T(8,128)(2,1)} fusion(bf16[512,2048]{1,0:T(8,128)(2,1)} %get-tuple-element.86.left_ref, bf16[512,2048]{1,0:T(8,128)(2,1)} %get-tuple-element.77.left_ref, bf16[512,2048]{1,0:T(8,128)(2,1)} %get-tuple-element.76.left_ref, bf16[512,2048]{1,0:T(8,128)(2,1)} %get-tuple-element.95.left_ref, ...), kind=kOutput, calls=%fused_computation.44 | convolution fusion | flops 17251172352 | bytes 25165824 | tf_op jit(solution)/shard_map/dot_general | solution.py:34
  578.5 17.2 %sums.11 = f32[512,2048]{1,0:T(8,128)} custom-call(bf16[512,4096]{1,0:T(8,128)(2,1)} %get-tuple-element.69.left_ref, bf16[2048,4096]{1,0:T(8,128)(2,1)} %all-gather.11.cloned.1.call-done.gate_ref.up_ref.right_ref), custom_call_target="tpu_custom_call" | custom-call | flops 1073741824 | bytes 1048576 | tf_op jit(solution)/shard_map/sums/pallas_call | solution.py:475
  605.8 43.2 %fusion.12 = bf16[2048,4096]{1,0:T(8,128)(2,1)} fusion(bf16[512,4096]{1,0:T(8,128)(2,1)} %get-tuple-element.74.left_ref, bf16[512,4096]{1,0:T(8,128)(2,1)} %get-tuple-element.66.left_ref, bf16[512,4096]{1,0:T(8,128)(2,1)} %get-tuple-element.65.left_ref, bf16[512,4096]{1,0:T(8,128)(2,1)} %get-tuple-element.69.left_ref, bf16[2048,2048]{1,0:T(8,128)(2,1)} %fusion.142), kind=kOutput, calls=%fused_computation.13 | convolution fusion | flops 34435235840 | bytes 41943040 | tf_op jit(solution)/shard_map/dot_general | solution.py:34
  700.3 21.2 %collective-permute-done.15 = bf16[128,2048]{1,0:T(8,128)(2,1)S(1)} collective-permute-done((bf16[128,2048]{1,0:T(8,128)(2,1)S(1)}, bf16[128,2048]{1,0:T(8,128)(2,1)S(1)}, u32[]{:S(2)}, u32[]{:S(2)}) %collective-permute-start.15) | collective-permute-done | bytes 524320 | tf_op jit(solution)/shard_map/ppermute | solution.py:504
  728.1 26.9 %attend_back.2 = bf16[512,4608]{1,0:T(8,128)(2,1)} custom-call(bf16[512,1536]{1,0:T(8,128)(2,1)} %get-tuple-element.78.q_ref, bf16[512,1536]{1,0:T(8,128)(2,1)} %get-tuple-element.79.k_ref, bf16[512,1536]{1,0:T(8,128)(2,1)} %get-tuple-element.80.v_ref, bf16[512,1536]{1,0:T(8,128)(2,1)} %fusion.66.g_ref, f32[512,128]{1,0:T(8,128)} %get-tuple-element.182.cos_ref, ...), custom_call_target="tpu_custom_call" | custom-call | flops 8053063680 | bytes 11010048 | tf_op jit(solution)/shard_map/attend_back/pallas_call | solution.py:407
  765.9 32.4 %collective-permute-done.18 = bf16[256,2048]{1,0:T(8,128)(2,1)S(1)} collective-permute-done((bf16[256,2048]{1,0:T(8,128)(2,1)S(1)}, bf16[256,2048]{1,0:T(8,128)(2,1)S(1)}, u32[]{:S(2)}, u32[]{:S(2)}) %collective-permute-start.18) | collective-permute-done | bytes 1048608 | tf_op jit(solution)/shard_map/ppermute | solution.py:504
  835.9 16.6 %fusion.8 = f32[512,2048]{1,0:T(8,128)} fusion(bf16[512,4608]{1,0:T(8,128)(2,1)} %attend_back.2, bf16[2048,6144]{1,0:T(8,128)(2,1)} %all-gather.9.cloned.1.call-done), kind=kOutput, calls=%fused_computation.9 | convolution fusion | flops 9663676416 | bytes 27787264 | tf_op jit(solution)/shard_map/dot_general | solution.py:40
  934.9 29.2 %collective-permute-done.37 = f32[2,2048]{1,0:T(2,128)S(1)} collective-permute-done((f32[2,2048]{1,0:T(2,128)S(1)}, f32[2,2048]{1,0:T(2,128)S(1)}, u32[]{:S(2)}, u32[]{:S(2)}) %collective-permute-start.37) | collective-permute-done | bytes 16416 | tf_op jit(solution)/shard_map/ppermute | solution.py:552
  979.5 21.1 %collective-permute-done.39 = f32[2,2048]{1,0:T(2,128)S(1)} collective-permute-done((f32[2,2048]{1,0:T(2,128)S(1)}, f32[2,2048]{1,0:T(2,128)S(1)}, u32[]{:S(2)}, u32[]{:S(2)}) %collective-permute-start.39) | collective-permute-done | bytes 16416 | tf_op jit(solution)/shard_map/ppermute | solution.py:552
  (301 shorter events, 400.2 us)
Async XLA Ops:
  7.2 104.5 %all-gather.7.cloned.1.call-start = ((), (), s32[]{:S(2)}) async-start(), calls=%async_computation.2 | async-start | bytes 9437184 | tf_op jit(solution)/shard_map/all_gather | solution.py:568
  12.2 205.0 %all-gather.9.cloned.1.call-start = ((), (), s32[]{:S(2)}) async-start(), calls=%async_computation.3 | async-start | bytes 28311552 | tf_op jit(solution)/shard_map/all_gather | solution.py:573
  94.1 275.9 %all-gather.13.cloned.1.call-start = ((), (), s32[]{:S(2)}) async-start(), calls=%async_computation.5 | async-start | bytes 9437184 | tf_op jit(solution)/shard_map/all_gather | solution.py:577
  94.8 275.1 %all-gather.11.cloned.1.call-start = ((), (), s32[]{:S(2)}) async-start(), calls=%async_computation.4 | async-start | bytes 18874368 | tf_op jit(solution)/shard_map/all_gather | solution.py:576
  98.1 627.2 %reduce-scatter.3.cloned.1.call-start = ((), (), s32[]{:S(2)}) async-start(), calls=%async_computation.6 | async-start | bytes 9437184 | tf_op jit(solution)/shard_map/reduce_scatter | solution.py:628
  107.8 50.0 %collective-permute-start.3 = (bf16[512,2048]{1,0:T(8,128)(2,1)}, bf16[512,2048]{1,0:T(8,128)(2,1)}, u32[]{:S(2)}, u32[]{:S(2)}) collective-permute-start(bf16[512,2048]{1,0:T(8,128)(2,1)} %grad_ref.1), channel_id=1, source_target_pairs={{0,1},{1,2},{2,3},{3,0},{4,5},{5,6},{6,7},{7,4},{8,9},{9,10},{10,1... | collective-permute-start | bytes 6291464 | tf_op jit(solution)/shard_map/ppermute | solution.py:492
  157.9 49.1 %collective-permute-start.4 = (bf16[512,2048]{1,0:T(8,128)(2,1)}, bf16[512,2048]{1,0:T(8,128)(2,1)}, u32[]{:S(2)}, u32[]{:S(2)}) collective-permute-start(bf16[512,2048]{1,0:T(8,128)(2,1)} %collective-permute-done.3.grad_ref), channel_id=1, source_target_pairs={{0,1},{1,2},{2,3},{3,0},{4,5},{5,6},{6,7},{7,4},{8,9},{9,10},{10,1... | collective-permute-start | bytes 6291464 | tf_op jit(solution)/shard_map/ppermute | solution.py:492
  207.0 60.5 %collective-permute-start.5 = (bf16[512,2048]{1,0:T(8,128)(2,1)}, bf16[512,2048]{1,0:T(8,128)(2,1)}, u32[]{:S(2)}, u32[]{:S(2)}) collective-permute-start(bf16[512,2048]{1,0:T(8,128)(2,1)} %collective-permute-done.4.grad_ref), channel_id=1, source_target_pairs={{0,1},{1,2},{2,3},{3,0},{4,5},{5,6},{6,7},{7,4},{8,9},{9,10},{10,1... | collective-permute-start | bytes 6291464 | tf_op jit(solution)/shard_map/ppermute | solution.py:492
  270.1 49.6 %collective-permute-start.6 = (bf16[512,2048]{1,0:T(8,128)(2,1)S(1)}, bf16[512,2048]{1,0:T(8,128)(2,1)S(1)}, u32[]{:S(2)}, u32[]{:S(2)}) collective-permute-start(bf16[512,2048]{1,0:T(8,128)(2,1)S(1)} %multiply_convert_fusion.norm_ref), channel_id=1, source_target_pairs={{0,1},{1,2},{2,3},{3,0},{4,5},{5,6},{6,7},{7,4},{8,9},{9,10},{10,1... | collective-permute-start | bytes 6291464 | tf_op jit(solution)/shard_map/ppermute | solution.py:492
  321.1 48.9 %collective-permute-start.7 = (bf16[512,2048]{1,0:T(8,128)(2,1)S(1)}, bf16[512,2048]{1,0:T(8,128)(2,1)}, u32[]{:S(2)}, u32[]{:S(2)}) collective-permute-start(bf16[512,2048]{1,0:T(8,128)(2,1)S(1)} %collective-permute-done.6.norm_ref), channel_id=1, source_target_pairs={{0,1},{1,2},{2,3},{3,0},{4,5},{5,6},{6,7},{7,4},{8,9},{9,10},{10,1... | collective-permute-start | bytes 6291464 | tf_op jit(solution)/shard_map/ppermute | solution.py:492
  410.4 50.6 %collective-permute-start.8 = (bf16[512,2048]{1,0:T(8,128)(2,1)}, bf16[512,2048]{1,0:T(8,128)(2,1)}, u32[]{:S(2)}, u32[]{:S(2)}) collective-permute-start(bf16[512,2048]{1,0:T(8,128)(2,1)} %convert_element_type.224), channel_id=1, source_target_pairs={{0,1},{1,2},{2,3},{3,0},{4,5},{5,6},{6,7},{7,4},{8,9},{9,10},{10,1... | collective-permute-start | bytes 6291464 | tf_op jit(solution)/shard_map/ppermute | solution.py:492
  410.5 95.4 %collective-permute-start.10 = (bf16[512,2048]{1,0:T(8,128)(2,1)}, bf16[512,2048]{1,0:T(8,128)(2,1)S(1)}, u32[]{:S(2)}, u32[]{:S(2)}) collective-permute-start(bf16[512,2048]{1,0:T(8,128)(2,1)} %collective-permute-done.7.norm_ref), channel_id=1, source_target_pairs={{0,1},{1,2},{2,3},{3,0},{4,5},{5,6},{6,7},{7,4},{8,9},{9,10},{10,1... | collective-permute-start | bytes 6291464 | tf_op jit(solution)/shard_map/ppermute | solution.py:492
  466.0 82.6 %collective-permute-start.9 = (bf16[512,2048]{1,0:T(8,128)(2,1)}, bf16[512,2048]{1,0:T(8,128)(2,1)}, u32[]{:S(2)}, u32[]{:S(2)}) collective-permute-start(bf16[512,2048]{1,0:T(8,128)(2,1)} %add_convert_fusion.7), channel_id=1, source_target_pairs={{0,1},{1,2},{2,3},{3,0},{4,5},{5,6},{6,7},{7,4},{8,9},{9,10},{10,1... | collective-permute-start | bytes 6291464 | tf_op jit(solution)/shard_map/ppermute | solution.py:492
  576.6 341.1 %reduce-scatter.5.cloned.1.call-start = ((), (), s32[]{:S(2)}) async-start(), calls=%async_computation.7 | async-start | bytes 18874368 | tf_op jit(solution)/shard_map/reduce_scatter | solution.py:628
  605.6 46.9 %collective-permute-start.11 = (bf16[512,2048]{1,0:T(8,128)(2,1)}, bf16[512,2048]{1,0:T(8,128)(2,1)}, u32[]{:S(2)}, u32[]{:S(2)}) collective-permute-start(bf16[512,2048]{1,0:T(8,128)(2,1)} %add_convert_fusion.6), channel_id=1, source_target_pairs={{0,1},{1,2},{2,3},{3,0},{4,5},{5,6},{6,7},{7,4},{8,9},{9,10},{10,1... | collective-permute-start | bytes 6291464 | tf_op jit(solution)/shard_map/ppermute | solution.py:492
  690.0 65.0 %collective-permute-start.12 = (bf16[512,2048]{1,0:T(8,128)(2,1)}, bf16[512,2048]{1,0:T(8,128)(2,1)S(1)}, u32[]{:S(2)}, u32[]{:S(2)}) collective-permute-start(bf16[512,2048]{1,0:T(8,128)(2,1)} %sums.12), channel_id=1, source_target_pairs={{0,1},{1,2},{2,3},{3,0},{4,5},{5,6},{6,7},{7,4},{8,9},{9,10},{10,1... | collective-permute-start | bytes 6291464 | tf_op jit(solution)/shard_map/ppermute | solution.py:492
  765.2 87.3 %collective-permute-start.19 = (bf16[1024,4608]{1,0:T(8,128)(2,1)}, bf16[1024,4608]{1,0:T(8,128)(2,1)}, u32[]{:S(2)}, u32[]{:S(2)}) collective-permute-start(bf16[1024,4608]{1,0:T(8,128)(2,1)} %convolution_convert_fusion), channel_id=1, source_target_pairs={{0,4},{4,0},{8,12},{12,8},{16,20},{20,16},{24,28},{28,24},{1,5},{5... | collective-permute-start | bytes 28311560 | tf_op jit(solution)/shard_map/ppermute | solution.py:504
  866.0 39.5 %collective-permute-start.21 = (bf16[128,4608]{1,0:T(8,128)(2,1)}, bf16[128,4608]{1,0:T(8,128)(2,1)}, u32[]{:S(2)}, u32[]{:S(2)}) collective-permute-start(bf16[128,4608]{1,0:T(8,128)(2,1)} %get-tuple-element.128), channel_id=1, source_target_pairs={{0,8},{4,12},{8,0},{12,4},{16,24},{20,28},{24,16},{28,20},{1,9},{5... | collective-permute-start | bytes 3538952 | tf_op jit(solution)/shard_map/ppermute | solution.py:504
  867.6 38.0 %collective-permute-start.20 = (bf16[128,4608]{1,0:T(8,128)(2,1)}, bf16[128,4608]{1,0:T(8,128)(2,1)}, u32[]{:S(2)}, u32[]{:S(2)}) collective-permute-start(bf16[128,4608]{1,0:T(8,128)(2,1)} %get-tuple-element.130), channel_id=1, source_target_pairs={{0,16},{4,20},{8,24},{12,28},{16,0},{20,4},{24,8},{28,12},{1,17},{... | collective-permute-start | bytes 3538952 | tf_op jit(solution)/shard_map/ppermute | solution.py:504
  870.3 47.3 %collective-permute-start.16 = (bf16[512,2048]{1,0:T(8,128)(2,1)}, bf16[512,2048]{1,0:T(8,128)(2,1)}, u32[]{:S(2)}, u32[]{:S(2)}) collective-permute-start(bf16[512,2048]{1,0:T(8,128)(2,1)} %add_convert_fusion.5), channel_id=1, source_target_pairs={{0,1},{1,2},{2,3},{3,0},{4,5},{5,6},{6,7},{7,4},{8,9},{9,10},{10,1... | collective-permute-start | bytes 6291464 | tf_op jit(solution)/shard_map/ppermute | solution.py:492
  909.9 54.8 %collective-permute-start.24 = (bf16[256,4608]{1,0:T(8,128)(2,1)}, bf16[256,4608]{1,0:T(8,128)(2,1)}, u32[]{:S(2)}, u32[]{:S(2)}) collective-permute-start(bf16[256,4608]{1,0:T(8,128)(2,1)} %pad_maximum_fusion.1), channel_id=1, source_target_pairs={{0,16},{4,20},{8,24},{12,28},{16,0},{20,4},{24,8},{28,12},{1,17},{... | collective-permute-start | bytes 7077896 | tf_op jit(solution)/shard_map/ppermute | solution.py:504
  912.9 51.8 %collective-permute-start.23 = (bf16[256,4608]{1,0:T(8,128)(2,1)}, bf16[256,4608]{1,0:T(8,128)(2,1)}, u32[]{:S(2)}, u32[]{:S(2)}) collective-permute-start(bf16[256,4608]{1,0:T(8,128)(2,1)} %pad_maximum_fusion), channel_id=1, source_target_pairs={{0,8},{4,12},{8,0},{12,4},{16,24},{20,28},{24,16},{28,20},{1,9},{5... | collective-permute-start | bytes 7077896 | tf_op jit(solution)/shard_map/ppermute | solution.py:504
  923.0 80.0 %collective-permute-start.28 = (bf16[1024,1536]{1,0:T(8,128)(2,1)}, bf16[1024,1536]{1,0:T(8,128)(2,1)S(1)}, u32[]{:S(2)}, u32[]{:S(2)}) collective-permute-start(bf16[1024,1536]{1,0:T(8,128)(2,1)} %convolution_convert_fusion.1), channel_id=1, source_target_pairs={{0,4},{4,0},{8,12},{12,8},{16,20},{20,16},{24,28},{28,24},{1,5},{5... | collective-permute-start | bytes 9437192 | tf_op jit(solution)/shard_map/ppermute | solution.py:504
  933.7 93.0 %collective-permute-start.22 = (bf16[512,2048]{1,0:T(8,128)(2,1)}, bf16[512,2048]{1,0:T(8,128)(2,1)S(1)}, u32[]{:S(2)}, u32[]{:S(2)}) collective-permute-start(bf16[512,2048]{1,0:T(8,128)(2,1)} %add_convert_fusion.4), channel_id=1, source_target_pairs={{0,1},{1,2},{2,3},{3,0},{4,5},{5,6},{6,7},{7,4},{8,9},{9,10},{10,1... | collective-permute-start | bytes 6291464 | tf_op jit(solution)/shard_map/ppermute | solution.py:492
  (75 other events, 1107.0 us)
Sparse Core Ops, SparseCore 0:
  12.3 56.9 all-gather.6
  94.2 122.9 all-gather.8
  219.1 54.3 all-gather.12
  275.7 89.6 all-gather.10
  576.7 68.7 reduce-scatter.2
  649.2 135.7 reduce-scatter.4

commit v3 on v2

--- a/solution.py
+++ b/solution.py
@@ -516,11 +516,12 @@
     return near, far
 
 
-def corner_step(kept):
+def corner_step(kept, *stage):
     rows = kept.shape[0] // 4
     half = rows // 2
     mine, over_x, over_y, corner = [kept[k * rows : (k + 1) * rows] for k in range(4)]
-    from_y, from_x = peer(corner[:half], 4), peer(corner[half:], 2)
+    from_y = after(peer(corner[:half], 4), *stage)
+    from_x = after(peer(corner[half:], 2), *stage)
     over_x = jnp.concatenate([over_x[:half] + from_y, over_x[half:]], axis=0)
     over_y = jnp.concatenate([over_y[:half], over_y[half:] + from_x], axis=0)
     return mine, over_x, over_y
@@ -545,20 +546,10 @@
     return total
 
 
-def sum_all(values, axes):
-    for name, count in axes:
-        hop = 1
-        while hop < count:
-            values = values + lax.ppermute(values, name, [(i, i ^ hop) for i in range(count)])
-            hop *= 2
-    return values
-
-
 def token_parallel(
     tokens, w_query, w_key, w_value, w_output, attn_gain, w_gate, w_up, w_down, mlp_gain, cotangent
 ):
     count = lax.axis_size("tensor")
-    dp_count = lax.axis_size("dp")
     heads = w_query.shape[1]
     hidden_units = w_gate.shape[1]
     gains = lax.all_gather(jnp.stack([attn_gain, mlp_gain]), "dp", axis=0)
@@ -599,7 +590,7 @@
     activs, pres, norm_parts = [], [], []
     arrived = None
     for j in range(count):
-        earlier = (normed[2],) if j == 1 else (norm_total,) if j == 3 else ()
+        earlier = (normed[j + 1],) if j in (1, 2) else (norm_total,) if j == 3 else ()
         rows = after(normed[j], *earlier)
         activ, pre = hidden_units_pass(rows, cotangents[j], gate_up, down)
         norm_part = times_rows(pre, gate_up, jnp.float32)
@@ -641,9 +632,9 @@
     ).astype(jnp.bfloat16)
     output_near = contract_rows(near_branch, after(all_mixed, rest_grad))
     output_near = (output_near + peer(output_far, 1).astype(jnp.float32)).astype(jnp.bfloat16)
-    output_parts = corner_step(output_near)
     rest_grad = after(rest_grad, output_near, grad_down)
     rest_pre = attention_back(rest_query, rest_key, rest_value, rest_grad, cosine, sine)
+    output_parts = corner_step(output_near, rest_pre)
 
     def mlp_part(j, stage):
         return times_rows(after(activs[j], stage), down, jnp.bfloat16)
@@ -657,7 +648,7 @@
     output_sum = cross_step(*output_parts)
     rest_later = after(rest_pre, rest_far)
     grad_normed_one = contract_cols(rest_later, rest[:, : 3 * wide])
-    rest_later = after(rest_later, grad_normed_one, output_sum)
+    rest_later = after(rest_later, grad_normed_one)
     rest_near = contract_rows(near_one, rest_later) + peer(rest_far, 1).astype(jnp.float32)
     rest_near = rest_near.astype(jnp.bfloat16)
     rest_parts = corner_step(rest_near)
@@ -665,7 +656,7 @@
         after(grad_branch, rest_near), own[:, 3 * heads :], preferred_element_type=jnp.float32
     ).astype(jnp.bfloat16)
     own_pre = attention_back(own_query, own_key, own_value, own_grad, cosine, sine)
-    own_pre = after(own_pre, mlp_arrived, grad_gate_up, *rest_parts)
+    own_pre = after(own_pre, mlp_arrived, grad_gate_up, output_sum, *rest_parts)
     mlp_next = after(mlp_part(3, rest_far), own_pre)
     mlp_total = (mlp_arrived.astype(jnp.float32) + mlp_next).astype(jnp.bfloat16)
     mlp_total = shift(mlp_total, count).astype(jnp.float32) + mlp_part(0, rest_near)
@@ -691,12 +682,12 @@
     grad_output = ring_sum(
         [output_sum[:, j * heads : (j + 1) * heads].astype(jnp.float32) for j in range(count)], count
     )
-    gain_parts = sum_all(
-        jnp.stack([attn_gain_part, mlp_gain_part]), (("dp", dp_count), ("tensor", count))
-    )
-    piece = gain_parts.shape[1] // (dp_count * count)
-    place = (lax.axis_index("dp") * count + lax.axis_index("tensor")) * piece
-    gain_sums = lax.dynamic_slice_in_dim(gain_parts, place, piece, axis=1)
+    gain_sums = lax.psum_scatter(
+        jnp.stack([attn_gain_part, mlp_gain_part]),
+        ("dp", "tensor"),
+        scatter_dimension=1,
+        tiled=True,
+    )
     return (
         block_out,
         grad_tokens,

time: 1060 us -> 1040 us (0.981)
  waiting for transfers between devices: 454 us -> 423 us
  other arithmetic: 79.8 us -> 93.4 us
    ppermute x5 -> x0, waiting for transfers between devices: 50.3 us -> none  [sum_all(): lax.ppermute(values, name, [(i, i ^ hop) for i in range(count)])]
    unnamed x6 -> x8, waiting for transfers between devices: 0.76 us -> 29.3 us
    ppermute x21, waiting for transfers between devices: 331 us -> 320 us  [shift(): lax.ppermute(values, 'tensor', [(i, (i + 1) % count) for i in range(count)])]
    unnamed x119 -> x152, local copies, waits for them, and re-layouts: 18.9 us -> 22.1 us
  transfers between devices with their start and end apart: 47 -> 43, of which waited for: 23 -> 21; matrix products, arithmetic and copies ran while one was open for 22% -> 23% of each run, Pallas kernels for 22% -> 26%
where the time goes in v3:
time: 1040 us; the launch traced here: 1030 us
  waiting for transfers between devices  423 us (41%)
  Pallas kernels  265 us (25%)
  matrix products  171 us (16%)
  other arithmetic  93.4 us (9%)
  local copies, waits for them, and re-layouts  32.7 us (3%)
  starting transfers between devices  25.6 us (2%)
  between operations  15.3 us (1%)
    ppermute x21, waiting for transfers between devices, shift(): lax.ppermute(values, 'tensor', [(i, (i + 1) % count) for i in range(count)])  320 us
    pallas_call x8, Pallas kernels, times_rows(): pl.pallas_call(rows_kernel, grid=(width // TILE,), in_specs=[pl.BlockSpec...  109 us
    dot_general x8, matrix products, contract_rows(): lax.dot_general(left, right, (((0,), (0,)), ((), ())), preferred_element_...  95 us
    pallas_call x4, Pallas kernels, hidden_units_pass(): pl.pallas_call(unit_kernel, grid=(steps,), in_specs=[whole, whole, tile(0...  83.6 us
    ppermute x15, waiting for transfers between devices, peer(): return lax.ppermute(values, 'dp', [(i, i ^ hop) for i in range(PEERS)])  63.8 us
    dot_general x4, matrix products, contract_cols(): lax.dot_general(left, right, (((1,), (1,)), ((), ())), preferred_element_...  39 us
    pallas_call x2, Pallas kernels, attention_back(): pl.pallas_call(backward_kernel, grid=(columns // PAIR,), in_specs=[pair_b...  36.7 us
    pallas_call x2, Pallas kernels, attention(): pl.pallas_call(forward_kernel, grid=(pairs,), in_specs=[pair_block(0), pa...  35.7 us
  transfers between devices with their start and end apart: 43, of which 21 were waited for; matrix products, arithmetic and copies ran while one was open for 23% of the time, Pallas kernels for 26%

profile of v3, /device:TPU:0, one launch (start us, length us, event | category | flops | bytes accessed | tf_op | source)
XLA Modules:
  0.0 1034.1 jit_solution(9060728917221745740)
XLA Ops:
  15.3 25.4 %collective-permute-done = bf16[256,2048]{1,0:T(8,128)(2,1)S(1)} collective-permute-done((bf16[256,2048]{1,0:T(8,128)(2,1)}, bf16[256,2048]{1,0:T(8,128)(2,1)S(1)}, u32[]{:S(2)}, u32[]{:S(2)}) %collective-permute-start) | collective-permute-done | bytes 1048608 | tf_op jit(solution)/shard_map/ppermute | solution.py:492
  40.7 26.1 %collective-permute-done.1 = bf16[256,2048]{1,0:T(8,128)(2,1)S(1)} collective-permute-done((bf16[256,2048]{1,0:T(8,128)(2,1)S(1)}, bf16[256,2048]{1,0:T(8,128)(2,1)S(1)}, u32[]{:S(2)}, u32[]{:S(2)}) %collective-permute-start.1) | collective-permute-done | bytes 1048608 | tf_op jit(solution)/shard_map/ppermute | solution.py:492
  66.9 25.2 %collective-permute-done.2 = bf16[256,2048]{1,0:T(8,128)(2,1)S(1)} collective-permute-done((bf16[256,2048]{1,0:T(8,128)(2,1)S(1)}, bf16[256,2048]{1,0:T(8,128)(2,1)S(1)}, u32[]{:S(2)}, u32[]{:S(2)}) %collective-permute-start.2) | collective-permute-done | bytes 1048608 | tf_op jit(solution)/shard_map/ppermute | solution.py:492
  130.1 27.8 %collective-permute-done.3.grad_ref = bf16[512,2048]{1,0:T(8,128)(2,1)} collective-permute-done((bf16[512,2048]{1,0:T(8,128)(2,1)}, bf16[512,2048]{1,0:T(8,128)(2,1)}, u32[]{:S(2)}, u32[]{:S(2)}) %collective-permute-start.3) | collective-permute-done | bytes 2097184 | tf_op jit(solution)/shard_map/ppermute | solution.py:492
  162.9 44.1 %collective-permute-done.4.grad_ref = bf16[512,2048]{1,0:T(8,128)(2,1)} collective-permute-done((bf16[512,2048]{1,0:T(8,128)(2,1)}, bf16[512,2048]{1,0:T(8,128)(2,1)}, u32[]{:S(2)}, u32[]{:S(2)}) %collective-permute-start.4) | collective-permute-done | bytes 2097184 | tf_op jit(solution)/shard_map/ppermute | solution.py:492
  217.2 16.5 %fusion.10.q_ref.k_ref.v_ref = f32[512,4608]{1,0:T(8,128)} fusion(bf16[512,2048]{1,0:T(8,128)(2,1)} %fusion.52, bf16[2048,6144]{1,0:T(8,128)(2,1)} %all-gather.9.cloned.1.call-done), kind=kOutput, calls=%fused_computation.11 | convolution fusion | flops 9663676416 | bytes 30408704 | tf_op jit(solution)/shard_map/dot_general | solution.py:581
  233.7 25.8 %attend.3 = (bf16[512,1536]{1,0:T(8,128)(2,1)}, bf16[512,1536]{1,0:T(8,128)(2,1)}, bf16[512,1536]{1,0:T(8,128)(2,1)}, bf16[512,1536]{1,0:T(8,128)(2,1)}) custom-call(f32[512,4608]{1,0:T(8,128)} %fusion.10.q_ref.k_ref.v_ref, f32[512,4608]{1,0:T(8,128)} %fusion.10.q_ref.k_ref.v_ref, f32[512,4608]{1,0:T(8,128)} %fusion.10.q_ref.k_ref.v_ref, ...), custom_call_target="tpu_custom_call" | custom-call | flops 3221225472 | bytes 15728640 | tf_op jit(solution)/shard_map/attend/pallas_call | solution.py:389
  271.6 48.1 %collective-permute-done.6.norm_ref = bf16[512,2048]{1,0:T(8,128)(2,1)S(1)} collective-permute-done((bf16[512,2048]{1,0:T(8,128)(2,1)S(1)}, bf16[512,2048]{1,0:T(8,128)(2,1)S(1)}, u32[]{:S(2)}, u32[]{:S(2)}) %collective-permute-start.6) | collective-permute-done | bytes 2097184 | tf_op jit(solution)/shard_map/ppermute | solution.py:492
  321.1 48.9 %collective-permute-done.7.norm_ref = bf16[512,2048]{1,0:T(8,128)(2,1)} collective-permute-done((bf16[512,2048]{1,0:T(8,128)(2,1)S(1)}, bf16[512,2048]{1,0:T(8,128)(2,1)}, u32[]{:S(2)}, u32[]{:S(2)}) %collective-permute-start.7) | collective-permute-done | bytes 2097184 | tf_op jit(solution)/shard_map/ppermute | solution.py:492
  370.0 20.9 %units.4 = (bf16[512,2048]{1,0:T(8,128)(2,1)}, bf16[512,4096]{1,0:T(8,128)(2,1)}) custom-call(bf16[512,2048]{1,0:T(8,128)(2,1)} %copy-done.17, bf16[512,2048]{1,0:T(8,128)(2,1)} %collective-permute-done.3.grad_ref, bf16[2048,4096]{1,0:T(8,128)(2,1)} %all-gather.11.cloned.1.call-done.gate_ref.up_ref.right_ref, ...), custom_call_target="tpu_custom_call" | custom-call | flops 2147483648 | bytes 4194304 | tf_op jit(solution)/shard_map/units/pallas_call | solution.py:449
  390.9 15.8 %sums.8 = f32[512,2048]{1,0:T(8,128)} custom-call(bf16[512,4096]{1,0:T(8,128)(2,1)} %get-tuple-element.68.left_ref, bf16[2048,4096]{1,0:T(8,128)(2,1)} %all-gather.11.cloned.1.call-done.gate_ref.up_ref.right_ref), custom_call_target="tpu_custom_call" | custom-call | flops 1073741824 | bytes 1048576 | tf_op jit(solution)/shard_map/sums/pallas_call | solution.py:475
  420.6 20.9 %units.5 = (bf16[512,2048]{1,0:T(8,128)(2,1)}, bf16[512,4096]{1,0:T(8,128)(2,1)}) custom-call(bf16[512,2048]{1,0:T(8,128)(2,1)} %collective-permute-done.7.norm_ref, bf16[512,2048]{1,0:T(8,128)(2,1)} %collective-permute-done.4.grad_ref, bf16[2048,4096]{1,0:T(8,128)(2,1)} %all-gather.11.cloned.1.call-done.gate_ref.up_ref.right_ref, ...), custom_call_target="tpu_custom_call" | custom-call | flops 2147483648 | bytes 4194304 | tf_op jit(solution)/shard_map/units/pallas_call | solution.py:449
  469.0 21.0 %units.7 = (bf16[512,2048]{1,0:T(8,128)(2,1)}, bf16[512,4096]{1,0:T(8,128)(2,1)}) custom-call(bf16[512,2048]{1,0:T(8,128)(2,1)} %copy-done.6, bf16[512,2048]{1,0:T(8,128)(2,1)} %grad_ref.1, bf16[2048,4096]{1,0:T(8,128)(2,1)} %all-gather.11.cloned.1.call-done.gate_ref.up_ref.right_ref, ...), custom_call_target="tpu_custom_call" | custom-call | flops 2147483648 | bytes 4194304 | tf_op jit(solution)/shard_map/units/pallas_call | solution.py:449
  490.0 20.9 %units.6 = (bf16[512,2048]{1,0:T(8,128)(2,1)}, bf16[512,4096]{1,0:T(8,128)(2,1)}) custom-call(bf16[512,2048]{1,0:T(8,128)(2,1)} %collective-permute-done.9.norm_ref, bf16[512,2048]{1,0:T(8,128)(2,1)} %collective-permute-done.5.grad_ref, bf16[2048,4096]{1,0:T(8,128)(2,1)} %all-gather.11.cloned.1.call-done.gate_ref.up_ref.right_ref, ...), custom_call_target="tpu_custom_call" | custom-call | flops 2147483648 | bytes 4194304 | tf_op jit(solution)/shard_map/units/pallas_call | solution.py:449
  510.9 15.8 %sums.10 = f32[512,2048]{1,0:T(8,128)} custom-call(bf16[512,4096]{1,0:T(8,128)(2,1)} %get-tuple-element.78.left_ref, bf16[2048,4096]{1,0:T(8,128)(2,1)} %all-gather.11.cloned.1.call-done.gate_ref.up_ref.right_ref), custom_call_target="tpu_custom_call" | custom-call | flops 1073741824 | bytes 1048576 | tf_op jit(solution)/shard_map/sums/pallas_call | solution.py:475
  531.7 23.0 %fusion.37 = bf16[2048,2048]{1,0:T(8,128)(2,1)} fusion(bf16[512,2048]{1,0:T(8,128)(2,1)} %get-tuple-element.92.left_ref, bf16[512,2048]{1,0:T(8,128)(2,1)} %get-tuple-element.81.left_ref, bf16[512,2048]{1,0:T(8,128)(2,1)} %get-tuple-element.80.left_ref, bf16[512,2048]{1,0:T(8,128)(2,1)} %get-tuple-element.101.left_ref, ...), kind=kOutput, calls=%fused_computation.44 | convolution fusion | flops 17251172352 | bytes 25165824 | tf_op jit(solution)/shard_map/dot_general | solution.py:34
  557.4 16.9 %sums.11 = f32[512,2048]{1,0:T(8,128)} custom-call(bf16[512,4096]{1,0:T(8,128)(2,1)} %get-tuple-element.73.left_ref, bf16[2048,4096]{1,0:T(8,128)(2,1)} %all-gather.11.cloned.1.call-done.gate_ref.up_ref.right_ref), custom_call_target="tpu_custom_call" | custom-call | flops 1073741824 | bytes 1048576 | tf_op jit(solution)/shard_map/sums/pallas_call | solution.py:475
  581.1 42.8 %fusion.12 = bf16[2048,4096]{1,0:T(8,128)(2,1)} fusion(bf16[512,4096]{1,0:T(8,128)(2,1)} %get-tuple-element.78.left_ref, bf16[512,4096]{1,0:T(8,128)(2,1)} %get-tuple-element.70.left_ref, bf16[512,4096]{1,0:T(8,128)(2,1)} %get-tuple-element.68.left_ref, bf16[512,4096]{1,0:T(8,128)(2,1)} %get-tuple-element.73.left_ref, bf16[2048,2048]{1,0:T(8,128)(2,1)} %fusion.141), kind=kOutput, calls=%fused_computation.13 | convolution fusion | flops 34435235840 | bytes 41943040 | tf_op jit(solution)/shard_map/dot_general | solution.py:34
  680.8 26.6 %attend_back.2 = bf16[512,4608]{1,0:T(8,128)(2,1)} custom-call(bf16[512,1536]{1,0:T(8,128)(2,1)} %get-tuple-element.82.q_ref, bf16[512,1536]{1,0:T(8,128)(2,1)} %get-tuple-element.83.k_ref, bf16[512,1536]{1,0:T(8,128)(2,1)} %get-tuple-element.84.v_ref, bf16[512,1536]{1,0:T(8,128)(2,1)} %fusion.66.g_ref, f32[512,128]{1,0:T(8,128)} %get-tuple-element.190.cos_ref, ...), custom_call_target="tpu_custom_call" | custom-call | flops 8053063680 | bytes 11010048 | tf_op jit(solution)/shard_map/attend_back/pallas_call | solution.py:407
  732.4 24.4 %collective-permute-done.18 = bf16[256,2048]{1,0:T(8,128)(2,1)S(1)} collective-permute-done((bf16[256,2048]{1,0:T(8,128)(2,1)}, bf16[256,2048]{1,0:T(8,128)(2,1)S(1)}, u32[]{:S(2)}, u32[]{:S(2)}) %collective-permute-start.18) | collective-permute-done | bytes 1048608 | tf_op jit(solution)/shard_map/ppermute | solution.py:504
  763.6 17.2 %fusion.8 = f32[512,2048]{1,0:T(8,128)} fusion(bf16[512,4608]{1,0:T(8,128)(2,1)} %attend_back.2, bf16[2048,6144]{1,0:T(8,128)(2,1)} %all-gather.9.cloned.1.call-done), kind=kOutput, calls=%fused_computation.9 | convolution fusion | flops 9663676416 | bytes 27787264 | tf_op jit(solution)/shard_map/dot_general | solution.py:40
  878.4 26.6 %collective-permute-done.23 = bf16[256,4608]{1,0:T(8,128)(2,1)} collective-permute-done((bf16[256,4608]{1,0:T(8,128)(2,1)}, bf16[256,4608]{1,0:T(8,128)(2,1)}, u32[]{:S(2)}, u32[]{:S(2)}) %collective-permute-start.23) | collective-permute-done | bytes 2359328 | tf_op jit(solution)/shard_map/ppermute | solution.py:504
  918.3 39.2 %collective-permute-done.25 = bf16[256,1536]{1,0:T(8,128)(2,1)S(1)} collective-permute-done((bf16[256,1536]{1,0:T(8,128)(2,1)S(1)}, bf16[256,1536]{1,0:T(8,128)(2,1)S(1)}, u32[]{:S(2)}, u32[]{:S(2)}) %collective-permute-start.25) | collective-permute-done | bytes 786464 | tf_op jit(solution)/shard_map/ppermute | solution.py:492
  987.5 28.5 %reduce-scatter.10.cloned.1.call-done = f32[64,2]{1,0:T(8,128)} async-done(((f32[2048,2]{1,0:T(8,128)}), f32[64,2]{1,0:T(8,128)}) %reduce-scatter.10.cloned.1.call-update) | async-done | bytes 528
  (323 shorter events, 370.5 us)
Async XLA Ops:
  7.2 104.5 %all-gather.7.cloned.1.call-start = ((), (), s32[]{:S(2)}) async-start(), calls=%async_computation.3 | async-start | bytes 9437184 | tf_op jit(solution)/shard_map/all_gather | solution.py:559
  12.2 205.0 %all-gather.9.cloned.1.call-start = ((), (), s32[]{:S(2)}) async-start(), calls=%async_computation.4 | async-start | bytes 28311552 | tf_op jit(solution)/shard_map/all_gather | solution.py:564
  94.1 275.9 %all-gather.13.cloned.1.call-start = ((), (), s32[]{:S(2)}) async-start(), calls=%async_computation.6 | async-start | bytes 9437184 | tf_op jit(solution)/shard_map/all_gather | solution.py:568
  94.8 275.1 %all-gather.11.cloned.1.call-start = ((), (), s32[]{:S(2)}) async-start(), calls=%async_computation.5 | async-start | bytes 18874368 | tf_op jit(solution)/shard_map/all_gather | solution.py:567
  98.1 579.8 %reduce-scatter.6.cloned.1.call-start = ((), (), s32[]{:S(2)}) async-start(), calls=%async_computation.7 | async-start | bytes 9437184 | tf_op jit(solution)/shard_map/reduce_scatter | solution.py:619
  107.9 50.0 %collective-permute-start.3 = (bf16[512,2048]{1,0:T(8,128)(2,1)}, bf16[512,2048]{1,0:T(8,128)(2,1)}, u32[]{:S(2)}, u32[]{:S(2)}) collective-permute-start(bf16[512,2048]{1,0:T(8,128)(2,1)} %grad_ref.1), channel_id=1, source_target_pairs={{0,1},{1,2},{2,3},{3,0},{4,5},{5,6},{6,7},{7,4},{8,9},{9,10},{10,1... | collective-permute-start | bytes 6291464 | tf_op jit(solution)/shard_map/ppermute | solution.py:492
  157.9 49.1 %collective-permute-start.4 = (bf16[512,2048]{1,0:T(8,128)(2,1)}, bf16[512,2048]{1,0:T(8,128)(2,1)}, u32[]{:S(2)}, u32[]{:S(2)}) collective-permute-start(bf16[512,2048]{1,0:T(8,128)(2,1)} %collective-permute-done.3.grad_ref), channel_id=1, source_target_pairs={{0,1},{1,2},{2,3},{3,0},{4,5},{5,6},{6,7},{7,4},{8,9},{9,10},{10,1... | collective-permute-start | bytes 6291464 | tf_op jit(solution)/shard_map/ppermute | solution.py:492
  207.0 60.5 %collective-permute-start.5 = (bf16[512,2048]{1,0:T(8,128)(2,1)}, bf16[512,2048]{1,0:T(8,128)(2,1)}, u32[]{:S(2)}, u32[]{:S(2)}) collective-permute-start(bf16[512,2048]{1,0:T(8,128)(2,1)} %collective-permute-done.4.grad_ref), channel_id=1, source_target_pairs={{0,1},{1,2},{2,3},{3,0},{4,5},{5,6},{6,7},{7,4},{8,9},{9,10},{10,1... | collective-permute-start | bytes 6291464 | tf_op jit(solution)/shard_map/ppermute | solution.py:492
  270.2 49.6 %collective-permute-start.6 = (bf16[512,2048]{1,0:T(8,128)(2,1)S(1)}, bf16[512,2048]{1,0:T(8,128)(2,1)S(1)}, u32[]{:S(2)}, u32[]{:S(2)}) collective-permute-start(bf16[512,2048]{1,0:T(8,128)(2,1)S(1)} %multiply_convert_fusion.norm_ref), channel_id=1, source_target_pairs={{0,1},{1,2},{2,3},{3,0},{4,5},{5,6},{6,7},{7,4},{8,9},{9,10},{10,1... | collective-permute-start | bytes 6291464 | tf_op jit(solution)/shard_map/ppermute | solution.py:492
  321.1 48.9 %collective-permute-start.7 = (bf16[512,2048]{1,0:T(8,128)(2,1)S(1)}, bf16[512,2048]{1,0:T(8,128)(2,1)}, u32[]{:S(2)}, u32[]{:S(2)}) collective-permute-start(bf16[512,2048]{1,0:T(8,128)(2,1)S(1)} %collective-permute-done.6.norm_ref), channel_id=1, source_target_pairs={{0,1},{1,2},{2,3},{3,0},{4,5},{5,6},{6,7},{7,4},{8,9},{9,10},{10,1... | collective-permute-start | bytes 6291464 | tf_op jit(solution)/shard_map/ppermute | solution.py:492
  370.0 50.6 %collective-permute-start.9 = (bf16[512,2048]{1,0:T(8,128)(2,1)}, bf16[512,2048]{1,0:T(8,128)(2,1)}, u32[]{:S(2)}, u32[]{:S(2)}) collective-permute-start(bf16[512,2048]{1,0:T(8,128)(2,1)} %collective-permute-done.7.norm_ref), channel_id=1, source_target_pairs={{0,1},{1,2},{2,3},{3,0},{4,5},{5,6},{6,7},{7,4},{8,9},{9,10},{10,1... | collective-permute-start | bytes 6291464 | tf_op jit(solution)/shard_map/ppermute | solution.py:492
  409.1 54.0 %collective-permute-start.8 = (bf16[512,2048]{1,0:T(8,128)(2,1)S(1)}, bf16[512,2048]{1,0:T(8,128)(2,1)}, u32[]{:S(2)}, u32[]{:S(2)}) collective-permute-start(bf16[512,2048]{1,0:T(8,128)(2,1)S(1)} %convert_element_type.224), channel_id=1, source_target_pairs={{0,1},{1,2},{2,3},{3,0},{4,5},{5,6},{6,7},{7,4},{8,9},{9,10},{10,1... | collective-permute-start | bytes 6291464 | tf_op jit(solution)/shard_map/ppermute | solution.py:492
  468.1 58.6 %collective-permute-start.10 = (bf16[512,2048]{1,0:T(8,128)(2,1)}, bf16[512,2048]{1,0:T(8,128)(2,1)}, u32[]{:S(2)}, u32[]{:S(2)}) collective-permute-start(bf16[512,2048]{1,0:T(8,128)(2,1)} %add_convert_fusion.7), channel_id=1, source_target_pairs={{0,1},{1,2},{2,3},{3,0},{4,5},{5,6},{6,7},{7,4},{8,9},{9,10},{10,1... | collective-permute-start | bytes 6291464 | tf_op jit(solution)/shard_map/ppermute | solution.py:492
  554.7 304.0 %reduce-scatter.8.cloned.1.call-start = ((), (), s32[]{:S(2)}) async-start(), calls=%async_computation.8 | async-start | bytes 18874368 | tf_op jit(solution)/shard_map/reduce_scatter | solution.py:619
  580.9 47.5 %collective-permute-start.11 = (bf16[512,2048]{1,0:T(8,128)(2,1)}, bf16[512,2048]{1,0:T(8,128)(2,1)S(1)}, u32[]{:S(2)}, u32[]{:S(2)}) collective-permute-start(bf16[512,2048]{1,0:T(8,128)(2,1)} %add_convert_fusion.6), channel_id=1, source_target_pairs={{0,1},{1,2},{2,3},{3,0},{4,5},{5,6},{6,7},{7,4},{8,9},{9,10},{10,1... | collective-permute-start | bytes 6291464 | tf_op jit(solution)/shard_map/ppermute | solution.py:492
  643.8 372.2 %reduce-scatter.10.cloned.1.call-start = ((), (), s32[]{:S(2)}) async-start(), calls=%async_computation.9 | async-start | bytes 1081344
  659.4 51.7 %collective-permute-start.12 = (bf16[512,2048]{1,0:T(8,128)(2,1)}, bf16[512,2048]{1,0:T(8,128)(2,1)}, u32[]{:S(2)}, u32[]{:S(2)}) collective-permute-start(bf16[512,2048]{1,0:T(8,128)(2,1)} %sums.12), channel_id=1, source_target_pairs={{0,1},{1,2},{2,3},{3,0},{4,5},{5,6},{6,7},{7,4},{8,9},{9,10},{10,1... | collective-permute-start | bytes 6291464 | tf_op jit(solution)/shard_map/ppermute | solution.py:492
  718.7 74.6 %collective-permute-start.17 = (bf16[1024,4608]{1,0:T(8,128)(2,1)}, bf16[1024,4608]{1,0:T(8,128)(2,1)}, u32[]{:S(2)}, u32[]{:S(2)}) collective-permute-start(bf16[1024,4608]{1,0:T(8,128)(2,1)} %convolution_convert_fusion), channel_id=1, source_target_pairs={{0,4},{4,0},{8,12},{12,8},{16,20},{20,16},{24,28},{28,24},{1,5},{5... | collective-permute-start | bytes 28311560 | tf_op jit(solution)/shard_map/ppermute | solution.py:504
  809.5 49.2 %collective-permute-start.16 = (bf16[512,2048]{1,0:T(8,128)(2,1)}, bf16[512,2048]{1,0:T(8,128)(2,1)}, u32[]{:S(2)}, u32[]{:S(2)}) collective-permute-start(bf16[512,2048]{1,0:T(8,128)(2,1)} %add_convert_fusion.5), channel_id=1, source_target_pairs={{0,1},{1,2},{2,3},{3,0},{4,5},{5,6},{6,7},{7,4},{8,9},{9,10},{10,1... | collective-permute-start | bytes 6291464 | tf_op jit(solution)/shard_map/ppermute | solution.py:492
  852.9 52.1 %collective-permute-start.23 = (bf16[256,4608]{1,0:T(8,128)(2,1)}, bf16[256,4608]{1,0:T(8,128)(2,1)}, u32[]{:S(2)}, u32[]{:S(2)}) collective-permute-start(bf16[256,4608]{1,0:T(8,128)(2,1)} %pad_maximum_fusion), channel_id=1, source_target_pairs={{0,8},{4,12},{8,0},{12,4},{16,24},{20,28},{24,16},{28,20},{1,9},{5... | collective-permute-start | bytes 7077896 | tf_op jit(solution)/shard_map/ppermute | solution.py:504
  856.6 51.5 %collective-permute-start.24 = (bf16[256,4608]{1,0:T(8,128)(2,1)}, bf16[256,4608]{1,0:T(8,128)(2,1)}, u32[]{:S(2)}, u32[]{:S(2)}) collective-permute-start(bf16[256,4608]{1,0:T(8,128)(2,1)} %pad_maximum_fusion.1), channel_id=1, source_target_pairs={{0,16},{4,20},{8,24},{12,28},{16,0},{20,4},{24,8},{28,12},{1,17},{... | collective-permute-start | bytes 7077896 | tf_op jit(solution)/shard_map/ppermute | solution.py:504
  863.8 94.0 %collective-permute-start.28 = (bf16[1024,1536]{1,0:T(8,128)(2,1)}, bf16[1024,1536]{1,0:T(8,128)(2,1)}, u32[]{:S(2)}, u32[]{:S(2)}) collective-permute-start(bf16[1024,1536]{1,0:T(8,128)(2,1)} %convolution_convert_fusion.1), channel_id=1, source_target_pairs={{0,4},{4,0},{8,12},{12,8},{16,20},{20,16},{24,28},{28,24},{1,5},{5... | collective-permute-start | bytes 9437192 | tf_op jit(solution)/shard_map/ppermute | solution.py:504
  878.4 139.6 %collective-permute-start.22 = (bf16[512,2048]{1,0:T(8,128)(2,1)}, bf16[512,2048]{1,0:T(8,128)(2,1)}, u32[]{:S(2)}, u32[]{:S(2)}) collective-permute-start(bf16[512,2048]{1,0:T(8,128)(2,1)} %add_convert_fusion.4), channel_id=1, source_target_pairs={{0,1},{1,2},{2,3},{3,0},{4,5},{5,6},{6,7},{7,4},{8,9},{9,10},{10,1... | collective-permute-start | bytes 6291464 | tf_op jit(solution)/shard_map/ppermute | solution.py:492
  912.4 45.1 %collective-permute-start.25 = (bf16[256,1536]{1,0:T(8,128)(2,1)S(1)}, bf16[256,1536]{1,0:T(8,128)(2,1)S(1)}, u32[]{:S(2)}, u32[]{:S(2)}) collective-permute-start(bf16[256,1536]{1,0:T(8,128)(2,1)S(1)} %pad_maximum_fusion.7), channel_id=1, source_target_pairs={{0,1},{1,2},{2,3},{3,0},{4,5},{5,6},{6,7},{7,4},{8,9},{9,10},{10,1... | collective-permute-start | bytes 2359304 | tf_op jit(solution)/shard_map/ppermute | solution.py:492
  (86 other events, 1513.3 us)
Sparse Core Ops, SparseCore 0:
  12.3 56.9 all-gather.6
  94.2 122.9 all-gather.8
  219.1 54.3 all-gather.12
  275.8 89.6 all-gather.10
  554.9 71.9 reduce-scatter.5
  643.9 137.1 reduce-scatter.7
  874.1 141.7 reduce-scatter.9
